TPU v7x, 256 devices: a whole 4x4x8 slice. The times are simulated.
256 devices in a mesh: ctx: 16 (over z, core), ch: 16 (over x, y).
Axes of the slice: x: 4, y: 4, z: 8, core: 2. Of those that a mesh axis runs over, the one named last changes fastest.
Arguments:
- layer_input: bfloat16 [6144, 16384], P('ctx', 'ch'), may hold values from -6 to 6
- gate_input: bfloat16 [6144, 16384], P('ctx', 'ch'), may hold values from -6 to 6
- conv_weight: float32 [4, 16384], P(None, 'ch'), may hold values from -3 to 3
- conv_bias: float32 [16384], P('ch'), may hold values from -3 to 3
- select_weight: bfloat16 [544, 16384], P(None, 'ch'), may hold values from -0.046875 to 0.046875
- step_weight: bfloat16 [512, 16384], P(None, 'ch'), may hold values from -0.25 to 0.25
- step_bias: float32 [16384], P('ch')
- decay_log: float32 [16, 16384], P(None, 'ch')
- skip_gain: float32 [16384], P('ch'), may hold values from 0.5 to 1.5
- out_weight: bfloat16 [16384, 4096], P('ch'), may hold values from -0.046875 to 0.046875
- residual: bfloat16 [6144, 4096], P('ctx', 'ch')
- norm_gain: float32 [4096], replicated, may hold values from 0.5 to 1.5
- head_weight: bfloat16 [4096, 32768], P('ctx', 'ch')
- targets: int32 [6144], P('ctx'), may hold values from 0 to 32767
Outputs:
- token_logprob: float32 [6144], P('ctx')
- mean_logprob: float32 [6144], P('ctx')
- logprob_variance: float32 [6144], P('ctx')
All inputs are finite; a program needn't handle non-finite values.
Results may differ from a plain program's by a relative error of at most 0.0051.
Values may be sent and summed in bfloat16 or wider, within the bound.
A program may use at most 128 MiB of HBM per device.

v0:
```python
import jax
import jax.numpy as jnp
from jax import lax
from jax.sharding import PartitionSpec as P

STATE = 16
RANK = 512
KCONV = 4


def from_behind(shard, axis, by):
    size = lax.axis_size(axis)
    pairs = [(i, i + by) for i in range(size) if 0 <= i + by < size]
    return lax.ppermute(shard, axis, pairs)


def sigmoid_linear(operand):
    return operand / (1.0 + jnp.exp(-operand))


def smooth_relu(operand):
    return jnp.logaddexp(operand, 0.0)


def per_device(
    layer_input,
    gate_input,
    conv_weight,
    conv_bias,
    select_weight,
    step_weight,
    step_bias,
    decay_log,
    skip_gain,
    out_weight,
    residual,
    norm_gain,
    head_weight,
    targets,
):
    tok_rows, channels = layer_input.shape
    edge_rows = from_behind(layer_input[tok_rows - (KCONV - 1) :], "ctx", 1)
    padded = jnp.concatenate([edge_rows, layer_input], axis=0).astype(jnp.float32)
    convolved = jnp.zeros((tok_rows, channels), jnp.float32) + conv_bias[None, :]
    for offset in range(KCONV):
        convolved = convolved + conv_weight[offset][None, :] * padded[offset : offset + tok_rows]
    smoothed = sigmoid_linear(convolved).astype(jnp.bfloat16)
    partial_sums = lax.dot_general(
        select_weight, smoothed, (((1,), (1,)), ((), ())), preferred_element_type=jnp.float32
    )
    projected = lax.psum(partial_sums, "ch")
    step_low = projected[:RANK].astype(jnp.bfloat16)
    state_entry = projected[RANK : RANK + STATE]
    state_readout = projected[RANK + STATE :]
    step_raw = lax.dot_general(
        step_low, step_weight, (((0,), (0,)), ((), ())), preferred_element_type=jnp.float32
    )
    step_size = smooth_relu(step_raw + step_bias[None, :])
    decay_rate = -jnp.exp(decay_log)
    smoothed_wide = smoothed.astype(jnp.float32)

    def advance(loop_carry, inputs):
        state_now, elapsed = loop_carry
        size_now, value_now, entry_now, readout_now = inputs
        state_now = (
            jnp.exp(size_now[None, :] * decay_rate) * state_now
            + (size_now * value_now)[None, :] * entry_now[:, None]
        )
        elapsed = elapsed + size_now
        return ((state_now, elapsed), (jnp.sum(readout_now[:, None] * state_now, axis=0), elapsed))

    start_carry = (jnp.zeros((STATE, channels), jnp.float32), jnp.zeros((channels,), jnp.float32))
    final_carry, outputs = lax.scan(
        advance, start_carry, (step_size, smoothed_wide, state_entry.T, state_readout.T), unroll=16
    )
    local_state, elapsed_total = final_carry
    scanned, elapsed = outputs
    through = jnp.exp(decay_rate * elapsed_total[None, :])

    def relay_step(step_index, incoming):
        return from_behind(through * incoming + local_state, "ctx", 1)

    incoming = lax.fori_loop(0, lax.axis_size("ctx") - 1, relay_step, jnp.zeros_like(local_state))
    correction = jnp.zeros_like(scanned)
    for index_state in range(STATE):
        correction = (
            correction
            + state_readout[index_state][:, None]
            * jnp.exp(decay_rate[index_state][None, :] * elapsed)
            * incoming[index_state][None, :]
        )
    mixer_input = (
        (scanned + correction + skip_gain[None, :] * smoothed_wide)
        * sigmoid_linear(gate_input.astype(jnp.float32))
    ).astype(jnp.bfloat16)
    mixer_out = lax.psum(jnp.dot(mixer_input, out_weight, preferred_element_type=jnp.float32), "ch")
    stream = lax.all_gather(residual, "ch", axis=1, tiled=True)
    hidden = stream.astype(jnp.float32) + mixer_out
    normed = (
        hidden
        * lax.rsqrt(jnp.mean(hidden * hidden, axis=1, keepdims=True) + 1e-06)
        * norm_gain[None, :]
    ).astype(jnp.bfloat16)
    vocab_cols = head_weight.shape[1]
    logits = jnp.dot(
        normed,
        lax.all_gather(head_weight, "ctx", axis=0, tiled=True),
        preferred_element_type=jnp.float32,
    )
    column = lax.broadcasted_iota(jnp.int32, logits.shape, 1) + lax.axis_index("ch") * vocab_cols
    picked = jnp.sum(jnp.where(column == targets[:, None], logits, 0.0), axis=1)
    row_peak = lax.pmax(jnp.max(logits, axis=1), "ch")
    shifted = logits - row_peak[:, None]
    weights = jnp.exp(shifted)
    row_total, row_first, row_second, picked = lax.psum(
        (
            jnp.sum(weights, axis=1),
            jnp.sum(weights * shifted, axis=1),
            jnp.sum(weights * shifted * shifted, axis=1),
            picked,
        ),
        "ch",
    )
    log_total = jnp.log(row_total)
    mean_ratio = row_first / row_total
    return (
        picked - row_peak - log_total,
        mean_ratio - log_total,
        row_second / row_total - mean_ratio * mean_ratio,
    )


def solution(mesh):
    in_specs = (
        P("ctx", "ch"),
        P("ctx", "ch"),
        P(None, "ch"),
        P("ch"),
        P(None, "ch"),
        P(None, "ch"),
        P("ch"),
        P(None, "ch"),
        P("ch"),
        P("ch", None),
        P("ctx", "ch"),
        P(),
        P("ctx", "ch"),
        P("ctx"),
    )
    out_specs = (P("ctx"), P("ctx"), P("ctx"))
    return jax.shard_map(
        per_device, mesh=mesh, in_specs=in_specs, out_specs=out_specs, check_vma=False
    )
```

profile of v0, /device:TPU:192, one launch (start us, length us, event | category | flops | bytes accessed | tf_op | source)
XLA Modules:
  0.0 683.5 jit_solution(6019642598044573003)
XLA Ops:
  10.8 2.2 collective-permute-done.1
  19.5 2.5 convert.6
  22.0 94.3 %all-reduce.4.cloned.1.call-done = f32[544,384]{1,0:T(8,128)} async-done(((f32[544,384]{1,0:T(8,128)}), f32[544,384]{1,0:T(8,128)}) %all-reduce.4.cloned.1.call-update) | async-done | bytes 835600 | tf_op jit(solution)/shard_map/psum | solution.py:51
  117.4 3.9 compare_select_fusion
  121.3 116.6 %while.28 = (s32[]{:T(128)}, f32[16,1024]{1,0:T(8,128)S(1)}, f32[1024]{0:T(1024)S(1)}, f32[24,16,1024]{2,1,0:T(8,128)}, f32[24,16,1024]{2,1,0:T(8,128)}, /*index...) while((s32[]{:T(128)}, f32[16,1024]{1,0:T(8,128)S(1)}, ...), condition=%wide.region_18.19_spmd.clone, body=%wide.region_1.18_spmd.clone.sunk | while | flops 2343954 | bytes 2588525 | solution.py:73
  239.4 91.0 %while.27 = (s32[]{:T(128)}, f32[16,1024]{1,0:T(8,128)S(1)}, f32[16,1024]{1,0:T(8,128)S(1)}, f32[16,1024]{1,0:T(8,128)S(1)}, s32[]{:T(128)}) while((s32[]{:T(128)}, f32[16,1024]{1,0:T(8,128)S(1)}, f32[16,1024]{1,0:T(8,128)S(1)}, f32[16,1024]{1,0:T(8,128)S(1)}, s32[]{:T(128)}) %tuple.214), condition=%wide.region_20.21_spmd, body=%wide.region_19.20_spmd.sunk | while | flops 32770 | bytes 524389 | solution.py:83
  239.4 1.9 collective-permute-start
  241.4 3.7 collective-permute-done
  245.0 1.9 collective-permute-start
  247.0 3.7 collective-permute-done
  252.6 3.7 collective-permute-done
  258.2 3.7 collective-permute-done
  263.8 3.7 collective-permute-done
  269.4 3.7 collective-permute-done
  275.0 3.7 collective-permute-done
  280.6 3.7 collective-permute-done
  286.2 3.7 collective-permute-done
  291.8 4.6 collective-permute-done
  298.3 4.9 collective-permute-done
  305.1 4.9 collective-permute-done
  311.9 4.9 collective-permute-done
  318.7 4.9 collective-permute-done
  325.5 4.9 collective-permute-done
  330.6 8.7 %fusion.111 = bf16[384,1024]{1,0:T(8,128)(2,1)S(1)} fusion(bf16[384,1024]{1,0:T(8,128)(2,1)} %param.19, f32[24,16,1024]{2,1,0:T(8,128)} %get-tuple-element.81, f32[24,16,1024]{2,1,0:T(8,128)} %get-tuple-element.80, f32[1024]{0:T(1024)S(1)} %copy-done.22, f32[1024]{0:T(1024)S(1)} %bitcast.639, f32[1024]{0:T(1024)S(1)} %bitcast.637, ...), kind=kLoop, calls=%fused_computation.241 | loop fusion | flops 33423360 | bytes 11190272 | tf_op jit(solution)/shard_map/convert_element_type | solution.py:95
  339.4 5.3 fusion.117
  345.3 142.4 %all-reduce.6.cloned.1.call-done = f32[384,4096]{1,0:T(8,128)} async-done(((f32[384,4096]{1,0:T(8,128)}), f32[384,4096]{1,0:T(8,128)}) %all-reduce.6.cloned.1.call-update) | async-done | bytes 6291472 | tf_op jit(solution)/shard_map/psum | solution.py:96
  487.6 4.6 multiply_reduce_fusion.16
  492.3 90.3 %all-gather.5.cloned.1.call-done = bf16[4096,2048]{1,0:T(8,128)(2,1)} async-done(((bf16[256,2048]{1,0:T(8,128)(2,1)}), bf16[4096,2048]{1,0:T(8,128)(2,1)}) %all-gather.5.cloned.1.call-update) | async-done | bytes 16777232 | tf_op jit(solution)/shard_map/all_gather | solution.py:107
  582.6 14.3 %fusion.116 = (f32[384]{0:T(512)S(1)}, f32[384,2048]{1,0:T(8,128)}) fusion(bf16[4096,2048]{1,0:T(8,128)(2,1)} %all-gather.5.cloned.1.call-done, f32[384,4096]{1,0:T(8,128)} %all-reduce.6.cloned.1.call-done, bf16[384,4096]{1,0:T(8,128)(2,1)} %all-gather.3.cloned.1.call-done, f32[4096]{0:T(1024)S(1)} %copy-done.20, f32[384]{0:T(512)S(1)} %add_rsqrt_fusion), kind=kOutput, calls=%fused_computation.274 | convolution fusion | flops 6451101184 | bytes 29379584 | tf_op jit(solution)/shard_map/dot_general | solution.py:105
  596.9 40.3 %pmax.7 = f32[384]{0:T(512)S(1)} all-reduce(f32[384]{0:T(512)S(1)} %get-tuple-element.335), channel_id=1, replica_groups=mesh['ctx'=16,'ch'=16] {'ch'}, use_global_device_ids=true, to_apply=%region_26.27 | all-reduce | flops 384 | bytes 3072 | tf_op jit(solution)/shard_map/pmax | solution.py:112
  637.2 3.2 fusion.35
  640.4 35.9 %all-reduce = (f32[384]{0:T(512)S(1)}, f32[384]{0:T(512)S(1)}, f32[384]{0:T(512)S(1)}, f32[384]{0:T(512)S(1)}) all-reduce(f32[384]{0:T(512)S(1)} %get-tuple-element.156, f32[384]{0:T(512)S(1)} %get-tuple-element.155, f32[384]{0:T(512)S(1)} %get-tuple-element.154, ...), channel_id=1, replica_groups=mesh['ctx'=16,'ch'=16] {'ch'}, use_global_device_ids=true, to_apply=%region_24.25 | all-reduce | flops 1536 | bytes 12288 | tf_op jit(solution)/shard_map/psum | solution.py:115
  (801 shorter events, 151.7 us)
Async XLA Ops:
  7.2 109.1 %all-reduce.4.cloned.1.call-start = ((), (), s32[]{:S(2)}) async-start(), calls=%async_computation.1 | async-start | bytes 1671168 | tf_op jit(solution)/shard_map/psum | solution.py:51
  8.0 5.0 collective-permute-start.1
  18.0 327.3 %all-gather.3.cloned.1.call-start = ((), (), s32[]{:S(2)}) async-start(), calls=%async_computation | async-start | bytes 3342336 | tf_op jit(solution)/shard_map/all_gather | solution.py:97
  18.7 468.9 %all-reduce.6.cloned.1.call-start = ((), (), s32[]{:S(2)}) async-start(), calls=%async_computation.2 | async-start | bytes 12582912 | tf_op jit(solution)/shard_map/psum | solution.py:96
  18.8 98.5 %copy-start.21 = (f32[1024]{0:T(1024)S(1)}, f32[1024]{0:T(1024)}, u32[]{:S(2)}) copy-start(f32[1024]{0:T(1024)} %param.24) | copy-start | bytes 12292
  237.9 92.5 %copy-start.5 = (f32[1,1024]{1,0:T(1,128)S(1)}, f32[1,1024]{1,0:T(1,128)}, u32[]{:S(2)}) copy-start(f32[1,1024]{1,0:T(1,128)} %get-tuple-element.299) | copy-start | bytes 12292
  237.9 92.5 %copy-start.6 = (f32[1,1024]{1,0:T(1,128)S(1)}, f32[1,1024]{1,0:T(1,128)}, u32[]{:S(2)}) copy-start(f32[1,1024]{1,0:T(1,128)} %get-tuple-element.300) | copy-start | bytes 12292
  238.0 92.5 %copy-start.7 = (f32[1,1024]{1,0:T(1,128)S(1)}, f32[1,1024]{1,0:T(1,128)}, u32[]{:S(2)}) copy-start(f32[1,1024]{1,0:T(1,128)} %get-tuple-element.301) | copy-start | bytes 12292
  238.0 92.5 %copy-start.8 = (f32[1,1024]{1,0:T(1,128)S(1)}, f32[1,1024]{1,0:T(1,128)}, u32[]{:S(2)}) copy-start(f32[1,1024]{1,0:T(1,128)} %get-tuple-element.302) | copy-start | bytes 12292
  238.0 92.5 %copy-start.9 = (f32[1,1024]{1,0:T(1,128)S(1)}, f32[1,1024]{1,0:T(1,128)}, u32[]{:S(2)}) copy-start(f32[1,1024]{1,0:T(1,128)} %get-tuple-element.303) | copy-start | bytes 12292
  238.0 92.5 %copy-start.10 = (f32[1,1024]{1,0:T(1,128)S(1)}, f32[1,1024]{1,0:T(1,128)}, u32[]{:S(2)}) copy-start(f32[1,1024]{1,0:T(1,128)} %get-tuple-element.304) | copy-start | bytes 12292
  238.0 92.5 %copy-start.11 = (f32[1,1024]{1,0:T(1,128)S(1)}, f32[1,1024]{1,0:T(1,128)}, u32[]{:S(2)}) copy-start(f32[1,1024]{1,0:T(1,128)} %get-tuple-element.305) | copy-start | bytes 12292
  238.0 92.5 %copy-start.12 = (f32[1,1024]{1,0:T(1,128)S(1)}, f32[1,1024]{1,0:T(1,128)}, u32[]{:S(2)}) copy-start(f32[1,1024]{1,0:T(1,128)} %get-tuple-element.306) | copy-start | bytes 12292
  238.0 92.5 %copy-start.13 = (f32[1,1024]{1,0:T(1,128)S(1)}, f32[1,1024]{1,0:T(1,128)}, u32[]{:S(2)}) copy-start(f32[1,1024]{1,0:T(1,128)} %get-tuple-element.307) | copy-start | bytes 12292
  239.4 5.6 collective-permute-start
  245.0 5.6 collective-permute-start
  250.7 5.6 collective-permute-start
  256.3 5.6 collective-permute-start
  261.9 5.6 collective-permute-start
  267.5 5.6 collective-permute-start
  273.1 5.6 collective-permute-start
  278.7 5.6 collective-permute-start
  284.3 5.6 collective-permute-start
  289.9 6.5 collective-permute-start
  296.4 6.8 collective-permute-start
  303.2 6.8 collective-permute-start
  310.0 6.8 collective-permute-start
  316.8 6.8 collective-permute-start
  323.6 6.8 collective-permute-start
  344.7 237.9 %all-gather.5.cloned.1.call-start = ((), (), s32[]{:S(2)}) async-start(), calls=%async_computation.3 | async-start | bytes 17825792 | tf_op jit(solution)/shard_map/all_gather | solution.py:107
  345.2 237.3 %copy-start.20 = (f32[4096]{0:T(1024)S(1)}, f32[4096]{0:T(1024)}, u32[]{:S(2)}) copy-start(f32[4096]{0:T(1024)} %param.29) | copy-start | bytes 49156
  492.3 144.9 %copy-start.18 = (s32[384]{0:T(512)S(1)}, s32[384]{0:T(512)}, u32[]{:S(2)}) copy-start(s32[384]{0:T(512)} %param.31) | copy-start | bytes 4612
  (11 other events, 583.7 us)
Sparse Core Ops, SparseCore 0:
  18.1 98.1 all-reduce.3
  118.7 56.0 all-gather.2
  344.8 142.8 all-reduce.5
  489.3 93.2 all-gather.4
where the time goes:
time: 694 us; the launch traced here: 683 us
  waiting for transfers between devices  392 us (56%)
  local copies, waits for them, and re-layouts  95.7 us (14%)
  blocking collectives  76.2 us (11%)
  other arithmetic  45 us (6%)
  starting transfers between devices  31.1 us (4%)
  matrix products  25.1 us (4%)
  between operations  14.2 us (2%)
    psum x1, waiting for transfers between devices, per_device(): lax.psum(jnp.dot(mixer_input, out_weight, preferred_element_type=jnp.floa...  142 us
    psum x1, waiting for transfers between devices, per_device(): projected = lax.psum(partial_sums, 'ch')  94.3 us
    all_gather x1, waiting for transfers between devices, per_device(): lax.all_gather(head_weight, 'ctx', axis=0, tiled=True)  90.3 us
    ppermute x16, waiting for transfers between devices, from_behind(): return lax.ppermute(shard, axis, pairs)  63.9 us
    slice x48, local copies, waits for them, and re-layouts, per_device(): lax.scan(advance, start_carry, (step_size, smoothed_wide, state_entry.T,...  63.6 us
    pmax x1, blocking collectives, per_device(): row_peak = lax.pmax(jnp.max(logits, axis=1), 'ch')  40.3 us
    psum x1, blocking collectives, per_device(): lax.psum((jnp.sum(weights, axis=1), jnp.sum(weights * shifted, axis=1), j...  35.9 us
    ppermute x16, starting transfers between devices, from_behind(): return lax.ppermute(shard, axis, pairs)  30.7 us
  transfers between devices with their start and end apart: 20, of which 19 were waited for; matrix products, arithmetic and copies ran while one was open for 21% of the time, Pallas kernels for 0%

commit v1 on v0

v1 whole, which is shorter than its diff:
```python
import functools

import jax
import jax.numpy as jnp
from jax import lax
from jax.experimental import pallas as pl
from jax.experimental.pallas import tpu as pltpu
from jax.sharding import PartitionSpec as P

STATE = 16
RANK = 512
KCONV = 4
TOK = 384
CH = 1024
D = 4096
VOC = 2048
NCH = 16
NZ = 8
LOG2E = 1.4426950408889634
MESH = pl.DeviceIdType.MESH
F32 = jnp.float32
BF16 = jnp.bfloat16
VM = pl.BlockSpec(memory_space=pltpu.VMEM)
SM = pl.BlockSpec(memory_space=pltpu.SMEM)
HBM = pl.BlockSpec(memory_space=pl.ANY)


def params(**kw):
    return pltpu.CompilerParams(vmem_limit_bytes=60 * 1024 * 1024, **kw)


def greet(peers):
    barrier = pltpu.get_barrier_semaphore()
    for peer in peers:
        pl.semaphore_signal(barrier, inc=1, device_id=peer, device_id_type=MESH)
    pl.semaphore_wait(barrier, len(peers))


def remote(src, dst, send_sem, recv_sem, peer):
    return pltpu.make_async_remote_copy(
        src_ref=src, dst_ref=dst, send_sem=send_sem, recv_sem=recv_sem, device_id=peer, device_id_type=MESH
    )


def sigmoid_linear(operand):
    return operand / (1.0 + jnp.exp(-operand))


ROWS = RANK // NCH


def sum_projected_kernel(part, bcpart, out, bc, recv, mine, recvx, minex, s1, r1, s2, r2, sx, rx, sy, ry):
    me = lax.axis_index("ch")
    others = [lax.rem(me + off, NCH) for off in range(1, NCH)]
    greet([{"ch": p} for p in others])
    first = []
    for k, p in enumerate(others):
        rows = pl.ds(pl.multiple_of(p * ROWS, ROWS), ROWS)
        c = remote(part.at[rows], recv.at[k], s1.at[k], r1.at[k], {"ch": p})
        c.start()
        first.append(c)

    def tile(k):
        slot = lax.rem(me - 5 * k + 2 * NCH, NCH) - 1
        return remote(bcpart.at[pl.ds(8 * k, 8)], recvx.at[slot], sx.at[k], rx.at[slot], {"ch": 5 * k})

    for k in range(4):
        @pl.when(me != 5 * k)
        def _():
            tile(k).start()

    myrows = pl.ds(pl.multiple_of(me * ROWS, ROWS), ROWS)
    for c in first:
        c.wait_recv()
    total = part[myrows].astype(F32)
    for k in range(NCH - 1):
        total = total + recv[k].astype(F32)
    mine[...] = total.astype(BF16)
    second = []
    for k, p in enumerate(others):
        c = remote(mine, out.at[myrows], s2.at[k], r2.at[k], {"ch": p})
        c.start()
        second.append(c)
    out[myrows] = mine[...]
    for k in range(4):
        def spread(j):
            return remote(minex, bc.at[pl.ds(8 * k, 8)], sy.at[j], ry.at[k], {"ch": lax.rem(me + j + 1, NCH)})

        @pl.when(me == 5 * k)
        def _():
            sumx = bcpart[8 * k : 8 * k + 8]
            for j in range(NCH - 1):
                remote(minex, recvx.at[j], sx.at[0], rx.at[j], {"ch": others[0]}).wait_recv()
                sumx = sumx + recvx[j]
            minex[...] = sumx
            for j in range(NCH - 1):
                spread(j).start()
            bc[8 * k : 8 * k + 8] = minex[...]

    for k in range(4):
        @pl.when(me != 5 * k)
        def _():
            tile(k).wait_send()
            remote(minex, bc.at[pl.ds(8 * k, 8)], sy.at[0], ry.at[k], {"ch": 5 * k}).wait_recv()

        @pl.when(me == 5 * k)
        def _():
            for j in range(NCH - 1):
                remote(minex, bc.at[pl.ds(8 * k, 8)], sy.at[j], ry.at[k], {"ch": others[j]}).wait_send()

    for c in second:
        c.wait_recv()
    for c in first:
        c.wait_send()
    for c in second:
        c.wait_send()


def sum_projected(part, bcpart):
    n = NCH - 1
    dma = pltpu.SemaphoreType.DMA
    return pl.pallas_call(
        sum_projected_kernel,
        out_shape=(jax.ShapeDtypeStruct(part.shape, BF16), jax.ShapeDtypeStruct(bcpart.shape, F32)),
        in_specs=[VM, VM],
        out_specs=(VM, VM),
        scratch_shapes=[
            pltpu.VMEM((n, ROWS, TOK), BF16),
            pltpu.VMEM((ROWS, TOK), BF16),
            pltpu.VMEM((n, 8, TOK), F32),
            pltpu.VMEM((8, TOK), F32),
            dma((n,)), dma((n,)), dma((n,)), dma((n,)), dma((4,)), dma((n,)), dma((n,)), dma((4,)),
        ],
        compiler_params=params(collective_id=0, has_side_effects=True),
        name="sum_projected",
    )(part, bcpart)


NTB = TOK // 8
FLAT = NTB * 64


def to_flat(ref, value, tok0):
    rows = value.shape[0]
    for b in range(rows // 8):
        for lt in range(8):
            start = (tok0 // 8 + b) * 64 + lt * 8
            ref[start : start + 8, :] = value[8 * b : 8 * b + 8, 128 * lt : 128 * lt + 128]


def scan_kernel(proj, step_w, bias, decay, smoothed, bc, y_out, e_out, state_out, total_out, dtf, uf):
    for k in range(TOK // 128):
        tok0 = 128 * k
        low = proj[:, tok0 : tok0 + 128]
        raw = lax.dot_general(low, step_w[...], (((0,), (0,)), ((), ())), preferred_element_type=F32)
        v = raw + bias[...]
        dt = jnp.maximum(v, 0.0) + jnp.log1p(jnp.exp(-jnp.abs(v)))
        to_flat(dtf, dt, tok0)
        to_flat(uf, dt * smoothed[tok0 : tok0 + 128, :].astype(F32), tok0)
    rates = [-jnp.exp(decay[8 * n : 8 * n + 8, :]) * LOG2E for n in range(STATE)]

    def block(tb, carry):
        state, elapsed = list(carry[:STATE]), carry[STATE]
        for r in range(8):
            rows = pl.ds(tb * 64 + r, 8, stride=8)
            dt = dtf[rows, :]
            u = uf[rows, :]
            t = tb * 8 + r
            y = None
            for n in range(STATE):
                state[n] = jnp.exp2(dt * rates[n]) * state[n] + u * bc[n, t]
                term = state[n] * bc[STATE + n, t]
                y = term if y is None else y + term
            elapsed = elapsed + dt
            y_out[rows, :] = y
            e_out[rows, :] = elapsed
        return (*state, elapsed)

    zero = jnp.zeros((8, 128), F32)
    last = lax.fori_loop(0, NTB, block, (zero,) * (STATE + 1))
    for n in range(STATE):
        state_out[8 * n : 8 * n + 8, :] = last[n]
    total_out[...] = last[STATE]


def local_scan(proj, step_w, bias, decay, smoothed, bc):
    shape = jax.ShapeDtypeStruct
    return pl.pallas_call(
        scan_kernel,
        out_shape=(shape((FLAT, 128), F32), shape((FLAT, 128), F32), shape((STATE * 8, 128), F32), shape((8, 128), F32)),
        in_specs=[VM, VM, VM, VM, VM, SM],
        out_specs=(VM, VM, VM, VM),
        scratch_shapes=[pltpu.VMEM((FLAT, 128), F32), pltpu.VMEM((FLAT, 128), F32)],
        compiler_params=params(),
        name="local_scan",
    )(proj, step_w, bias, decay, smoothed, bc)


HALF = STATE * 4


def carry_kernel(state, total, decay, out, swap_s, swap_e, got_s, got_e, send_s, send_e, zs, ze, hold, fin, ss, rs, sz, rz, sf, rf):
    me = lax.axis_index("ctx")
    z = me // 2
    c = lax.rem(me, 2)
    partner = {"ctx": z * 2 + 1 - c}
    greet([partner] + [{"ctx": lax.rem(z + d, NZ) * 2 + c} for d in range(1, NZ)])
    mine = pl.ds(pl.multiple_of(c * HALF, HALF), HALF)
    other = pl.ds(pl.multiple_of((1 - c) * HALF, HALF), HALF)
    swap_s[...] = state[other, :]
    swap_e[...] = total[...]
    a = remote(swap_s, got_s, ss.at[0], rs.at[0], partner)
    b = remote(swap_e, got_e, ss.at[1], rs.at[1], partner)
    a.start()
    b.start()
    rate = -jnp.exp(decay[mine, :]) * LOG2E

    def through(elapsed):
        return jnp.exp2(rate * jnp.tile(elapsed, (HALF // 8, 1)))

    a.wait_recv()
    b.wait_recv()
    own_s, own_e, oth_s, oth_e = state[mine, :], total[...], got_s[...], got_e[...]
    low = c == 0
    s0, s1 = jnp.where(low, own_s, oth_s), jnp.where(low, oth_s, own_s)
    e0, e1 = jnp.where(low, own_e, oth_e), jnp.where(low, oth_e, own_e)
    send_s[...] = (through(e1) * s0 + s1).astype(BF16)
    send_e[...] = e0 + e1

    def pair(d):
        peer = {"ctx": (z + d) * 2 + c}
        return (
            remote(send_s, zs.at[d - 1], sz.at[0, d - 1], rz.at[0, d - 1], peer),
            remote(send_e, ze.at[d - 1], sz.at[1, d - 1], rz.at[1, d - 1], peer),
        )

    def incoming(d):
        peer = {"ctx": (z - d) * 2 + c}
        return (
            remote(send_s, zs.at[d - 1], sz.at[0, d - 1], rz.at[0, d - 1], peer),
            remote(send_e, ze.at[d - 1], sz.at[1, d - 1], rz.at[1, d - 1], peer),
        )

    for d in range(1, NZ):
        @pl.when(z + d < NZ)
        def _():
            for copy in pair(d):
                copy.start()

    hold[...] = jnp.zeros_like(hold)
    for d in range(NZ - 1, 0, -1):
        @pl.when(z >= d)
        def _():
            for copy in incoming(d):
                copy.wait_recv()
            hold[...] = through(ze[d - 1]) * hold[...] + zs[d - 1].astype(F32)

    into0 = hold[...]
    into1 = through(e0) * into0 + s0
    fin[...] = jnp.where(low, into1, into0)
    out[mine, :] = jnp.where(low, into0, into1)
    f = remote(fin, out.at[mine], sf.at[0], rf.at[0], partner)
    f.start()
    f.wait_recv()
    f.wait_send()
    a.wait_send()
    b.wait_send()
    for d in range(1, NZ):
        @pl.when(z + d < NZ)
        def _():
            for copy in pair(d):
                copy.wait_send()


def carry_in(state, total, decay):
    dma = pltpu.SemaphoreType.DMA
    return pl.pallas_call(
        carry_kernel,
        out_shape=jax.ShapeDtypeStruct((STATE * 8, 128), F32),
        in_specs=[VM, VM, VM],
        out_specs=VM,
        scratch_shapes=[
            pltpu.VMEM((HALF, 128), F32),
            pltpu.VMEM((8, 128), F32),
            pltpu.VMEM((HALF, 128), F32),
            pltpu.VMEM((8, 128), F32),
            pltpu.VMEM((HALF, 128), BF16),
            pltpu.VMEM((8, 128), F32),
            pltpu.VMEM((NZ - 1, HALF, 128), BF16),
            pltpu.VMEM((NZ - 1, 8, 128), F32),
            pltpu.VMEM((HALF, 128), F32),
            pltpu.VMEM((HALF, 128), F32),
            dma((2,)), dma((2,)), dma((2, NZ - 1)), dma((2, NZ - 1)), dma((1,)), dma((1,)),
        ],
        compiler_params=params(collective_id=1, has_side_effects=True),
        name="carry_in",
    )(state, total, decay)


def gate_kernel(y, e, incoming, decay, bc, smoothed, gate, skip, out, zf):
    rates = [-jnp.exp(decay[8 * n : 8 * n + 8, :]) * LOG2E for n in range(STATE)]
    into = [incoming[8 * n : 8 * n + 8, :] for n in range(STATE)]

    def block(tb, _):
        for r in range(8):
            rows = pl.ds(tb * 64 + r, 8, stride=8)
            elapsed = e[rows, :]
            total = y[rows, :]
            t = tb * 8 + r
            for n in range(STATE):
                total = total + jnp.exp2(elapsed * rates[n]) * into[n] * bc[STATE + n, t]
            zf[rows, :] = total
        return 0

    lax.fori_loop(0, NTB, block, 0)
    for k in range(TOK // 16):
        rows = slice(16 * k, 16 * k + 16)
        for lt in range(8):
            lanes = slice(128 * lt, 128 * lt + 128)
            start = (2 * k) * 64 + lt * 8
            scanned = jnp.concatenate([zf[start : start + 8, :], zf[start + 64 : start + 72, :]], axis=0)
            value = scanned + skip[:, lanes] * smoothed[rows, lanes].astype(F32)
            out[rows, lanes] = (value * sigmoid_linear(gate[rows, lanes].astype(F32))).astype(BF16)


def gated(y, e, incoming, decay, bc, smoothed, gate, skip):
    return pl.pallas_call(
        gate_kernel,
        out_shape=jax.ShapeDtypeStruct((TOK, CH), BF16),
        in_specs=[VM, VM, VM, VM, SM, VM, VM, VM],
        out_specs=VM,
        scratch_shapes=[pltpu.VMEM((FLAT, 128), F32)],
        compiler_params=params(),
        name="gated",
    )(y, e, incoming, decay, bc, smoothed, gate, skip)


NQ = 4
QR = TOK // NQ
BLK = D // NCH


def cube_of(index):
    x, y = index // 4, lax.rem(index, 4)
    return [lax.rem(x + x // 2, 2), x // 2, lax.rem(y + y // 2, 2), y // 2]


def index_of(bits):
    def line(low, high):
        return high * 2 + lax.rem(high + low, 2)

    return line(bits[0], bits[1]) * 4 + line(bits[2], bits[3])


def mix_kernel(mixer, weight, residual, gain, out, wv, acc, part, got, ws, s1, r1, s2, r2):
    me = lax.axis_index("ch")
    bits = cube_of(me)

    def block(r):
        return index_of([lax.rem(bits[d] + ((r >> d) & 1), 2) for d in range(4)])

    def lanes(r):
        return pl.ds(pl.multiple_of(block(r) * BLK, BLK), BLK)

    order = [15, 14, 13, 11, 7, 12, 10, 9, 6, 5, 3, 8, 4, 2, 1, 0]
    loads = []
    for k in range(8):
        piece = pl.ds(CH // 8 * k, CH // 8)
        loads.append(pltpu.make_async_copy(weight.at[piece], wv.at[piece], ws.at[k]))
        loads[k].start()
    peers = [{"ch": block(1 << d)} for d in range(4)]
    greet(peers)

    def rows(q):
        return pl.ds(QR * q, QR)

    def dim(q, s):
        return (q + s) % 4

    def kept(q, s):
        return [r for r in range(16) if all(not (r >> dim(q, i)) & 1 for i in range(s))]

    sent = []

    def send(q, s, r):
        d = dim(q, s)
        c = remote(
            part.at[r, rows(q)], got.at[s, r ^ (1 << d), rows(q)], s1.at[r, q], r1.at[q, r ^ (1 << d), s], peers[d]
        )
        c.start()
        sent.append(c)

    def take(q, s, r):
        d = dim(q, s)
        remote(part.at[r, rows(q)], got.at[s, r, rows(q)], s1.at[r, q], r1.at[q, r, s], peers[d]).wait_recv()

    for load in loads:
        load.wait()
    for r in order:
        product = jnp.dot(mixer[...], wv[:, lanes(r)], preferred_element_type=F32)
        acc[r] = product
        part[r] = product.astype(BF16)
        for q in range(NQ):
            if (r >> dim(q, 0)) & 1:
                send(q, 0, r)
    for s in range(3):
        for q in range(NQ):
            left = kept(q, s + 1)
            d = dim(q, s + 1)
            for r in [r for r in left if (r >> d) & 1] + [r for r in left if not (r >> d) & 1]:
                take(q, s, r)
                total = acc[r, rows(q)] + got[s, r, rows(q)].astype(F32)
                if not (r >> d) & 1:
                    acc[r, rows(q)] = total
                else:
                    part[r, rows(q)] = total.astype(BF16)
                    send(q, s + 1, r)

    def give(q, s, r):
        d = dim(q, s)
        where = out.at[rows(q), lanes(r)]
        return remote(where, where, s2.at[q, s, r], r2.at[q, s, r ^ (1 << d)], peers[d])

    def spread(q, s):
        held = [0]
        for i in range(s):
            held = held + [r ^ (1 << dim(q, i)) for r in held]
        return held

    for q in range(NQ):
        take(q, 3, 0)
        total = acc[0, rows(q)] + got[3, 0, rows(q)].astype(F32)
        hidden = residual[rows(q), :].astype(F32) + total
        out[rows(q), lanes(0)] = (hidden * gain[:, lanes(0)]).astype(BF16)
        c = give(q, 0, 0)
        c.start()
        sent.append(c)

    def arrived(q, s, r):
        where = out.at[rows(q), lanes(r)]
        remote(where, where, s2.at[q, s, r], r2.at[q, s, r], peers[dim(q, s)]).wait_recv()

    for s in range(4):
        for q in range(NQ):
            for r in spread(q, s):
                arrived(q, s, r ^ (1 << dim(q, s)))
            if s < 3:
                for r in spread(q, s + 1):
                    c = give(q, s + 1, r)
                    c.start()
                    sent.append(c)
    for c in sent:
        c.wait_send()


def mix(mixer, weight, residual, gain):
    dma = pltpu.SemaphoreType.DMA
    return pl.pallas_call(
        mix_kernel,
        out_shape=jax.ShapeDtypeStruct((TOK, D), BF16),
        in_specs=[VM, HBM, VM, VM],
        out_specs=VM,
        scratch_shapes=[
            pltpu.VMEM((CH, D), BF16),
            pltpu.VMEM((NCH, TOK, BLK), F32),
            pltpu.VMEM((NCH, TOK, BLK), BF16),
            pltpu.VMEM((4, NCH, TOK, BLK), BF16),
            dma((8,)),
            dma((NCH, NQ)),
            dma((NQ, NCH, 4)),
            dma((NQ, 4, NCH)),
            dma((NQ, 4, NCH)),
        ],
        compiler_params=params(collective_id=2, has_side_effects=True),
        name="mix",
    )(mixer, weight, residual, gain)


VT = 256
NVT = VOC // VT


def score_kernel(scaled, head, gain, targets, out, logits, rms):
    step = pl.program_id(0)

    @pl.when(step == 0)
    def _():
        acc = jnp.zeros((TOK, BLK), F32)
        for k in range(D // BLK):
            lanes = slice(BLK * k, BLK * k + BLK)
            h = scaled[:, lanes].astype(F32) / gain[:, lanes]
            acc = acc + h * h
        mean = jnp.sum(acc, axis=1, keepdims=True) * (1.0 / D)
        rms[...] = lax.rsqrt(mean + 1e-06)

    logits[step] = jnp.dot(scaled[...], head[...], preferred_element_type=F32) * rms[...]

    @pl.when(step == NVT - 1)
    def _():
        first = lax.axis_index("ch") * VOC
        lane = lax.broadcasted_iota(jnp.int32, (32, VT), 1)
        place = lax.broadcasted_iota(jnp.int32, (32, 128), 1)
        for k in range(TOK // 32):
            rows = slice(32 * k, 32 * k + 32)
            values = [logits[j, rows] for j in range(NVT)]
            peak = values[0]
            for v in values[1:]:
                peak = jnp.maximum(peak, v)
            peak = jnp.max(peak, axis=1, keepdims=True)
            want = targets[rows, :] - first
            sums = [jnp.zeros((32, VT), F32) for _ in range(4)]
            for j, v in enumerate(values):
                shifted = v - peak
                w = jnp.exp(shifted)
                ws = w * shifted
                sums[0] = sums[0] + w
                sums[1] = sums[1] + ws
                sums[2] = sums[2] + ws * shifted
                sums[3] = sums[3] + jnp.where(lane + j * VT == want, v, 0.0)
            cols = [peak] + [jnp.sum(v, axis=1, keepdims=True) for v in sums]
            packed = jnp.zeros((32, 128), F32)
            for i, v in enumerate(cols):
                packed = jnp.where(place == i, v, packed)
            out[rows, :] = packed


def score(scaled, head, gain, targets):
    return pl.pallas_call(
        score_kernel,
        out_shape=jax.ShapeDtypeStruct((TOK, 128), F32),
        grid=(NVT,),
        in_specs=[
            pl.BlockSpec((TOK, D), lambda i: (0, 0)),
            pl.BlockSpec((D, VT), lambda i: (0, i)),
            pl.BlockSpec((1, D), lambda i: (0, 0)),
            pl.BlockSpec((TOK, 1), lambda i: (0, 0)),
        ],
        out_specs=pl.BlockSpec((TOK, 128), lambda i: (0, 0)),
        scratch_shapes=[pltpu.VMEM((NVT, TOK, VT), F32), pltpu.VMEM((TOK, 1), F32)],
        compiler_params=params(),
        name="score",
    )(scaled, head, gain, targets)


def combine_kernel(packed, out, mine, got, ss, rs):
    me = lax.axis_index("ch")
    others = [lax.rem(me + off, NCH) for off in range(1, NCH)]
    mine[...] = jnp.transpose(packed[...])[:8, :]
    greet([{"ch": p} for p in others])
    copies = []
    for k, p in enumerate(others):
        c = remote(mine, got.at[k], ss.at[k], rs.at[k], {"ch": p})
        c.start()
        copies.append(c)
    for c in copies:
        c.wait_recv()
    parts = [mine[...]] + [got[k] for k in range(NCH - 1)]
    peak = parts[0][0:1, :]
    for v in parts[1:]:
        peak = jnp.maximum(peak, v[0:1, :])
    total = first = second = picked = jnp.zeros((1, TOK), F32)
    for v in parts:
        d = v[0:1, :] - peak
        w = jnp.exp(d)
        wd = w * d
        total = total + w * v[1:2, :]
        first = first + (w * v[2:3, :] + wd * v[1:2, :])
        second = second + (w * v[3:4, :] + 2.0 * wd * v[2:3, :] + wd * d * v[1:2, :])
        picked = picked + v[4:5, :]
    log_total = jnp.log(total)
    ratio = first / total
    out[0:1, :] = picked - peak - log_total
    out[1:2, :] = ratio - log_total
    out[2:3, :] = second / total - ratio * ratio
    for c in copies:
        c.wait_send()


def combine(packed):
    dma = pltpu.SemaphoreType.DMA
    return pl.pallas_call(
        combine_kernel,
        out_shape=jax.ShapeDtypeStruct((8, TOK), F32),
        in_specs=[VM],
        out_specs=VM,
        scratch_shapes=[
            pltpu.VMEM((8, TOK), F32),
            pltpu.VMEM((NCH - 1, 8, TOK), F32),
            dma((NCH - 1,)),
            dma((NCH - 1,)),
        ],
        compiler_params=params(collective_id=3, has_side_effects=True),
        name="combine",
    )(packed)


def per_device(
    layer_input, gate_input, conv_weight, conv_bias, select_weight, step_weight, step_bias, decay_log,
    skip_gain, out_weight, residual, norm_gain, head_weight, targets,
):
    head = lax.all_gather(head_weight, "ctx", axis=0, tiled=True)
    size = lax.axis_size("ctx")
    edge = lax.ppermute(layer_input[TOK - (KCONV - 1) :], "ctx", [(i, i + 1) for i in range(size - 1)])
    padded = jnp.concatenate([edge, layer_input], axis=0).astype(F32)
    convolved = jnp.zeros((TOK, CH), F32) + conv_bias[None, :]
    for offset in range(KCONV):
        convolved = convolved + conv_weight[offset][None, :] * padded[offset : offset + TOK]
    smoothed = sigmoid_linear(convolved).astype(BF16)
    part = lax.dot_general(select_weight, smoothed, (((1,), (1,)), ((), ())), preferred_element_type=F32)
    proj, bc = sum_projected(part[:RANK].astype(BF16), part[RANK:])
    decay = decay_log.reshape(STATE * 8, 128)
    y, e, state, total = local_scan(proj, step_weight, step_bias[None, :], decay, smoothed, bc)
    incoming = carry_in(state, total, decay)
    mixer = gated(y, e, incoming, decay, bc, smoothed, gate_input, skip_gain[None, :])
    scaled = mix(mixer, out_weight, residual, norm_gain[None, :])
    packed = score(scaled, head, norm_gain[None, :], targets[:, None])
    result = combine(packed)
    return result[0], result[1], result[2]


def solution(mesh):
    in_specs = (
        P("ctx", "ch"), P("ctx", "ch"), P(None, "ch"), P("ch"), P(None, "ch"), P(None, "ch"), P("ch"),
        P(None, "ch"), P("ch"), P("ch", None), P("ctx", "ch"), P(), P("ctx", "ch"), P("ctx"),
    )
    return jax.shard_map(
        per_device, mesh=mesh, in_specs=in_specs, out_specs=(P("ctx"), P("ctx"), P("ctx")), check_vma=False
    )
```

time: 694 us -> 182 us (0.26); the launches traced: 683 us -> 181 us
  waiting for transfers between devices: 392 us -> 0.7 us
  Pallas kernels: 0 us -> 155 us
  local copies, waits for them, and re-layouts: 95.7 us -> 7.43 us
  blocking collectives: 76.2 us -> 0 us
  other arithmetic: 45 us -> 1.24 us
  starting transfers between devices: 31.1 us -> 1.95 us
  matrix products: 25.1 us -> 0.76 us
    psum x2 -> x0, waiting for transfers between devices: 237 us -> none  [the longest x1 142 us: per_device(): lax.psum(jnp.dot(mixer_input, out_weight, preferred_element_type=jnp.floa...]
    pallas_call x0 -> x7, Pallas kernels: none -> 155 us  [the longest x1 61.9 us: mix(): pl.pallas_call(mix_kernel, out_shape=jax.ShapeDtypeStruct((TOK, D), BF16)...]
    all_gather x2 -> x1, waiting for transfers between devices: 90.3 us -> 0.02 us  [per_device(): head = lax.all_gather(head_weight, 'ctx', axis=0, tiled=True)]
    ppermute x16 -> x1, waiting for transfers between devices: 63.9 us -> 0.01 us  [per_device(): lax.ppermute(layer_input[TOK - (KCONV - 1):], 'ctx', [(i, i + 1) for i in...]
    slice x53 -> x5, local copies, waits for them, and re-layouts: 67.3 us -> 4.46 us  [the longest x1 1.42 us: per_device(): return (result[0], result[1], result[2])]
    pmax x1 -> x0, blocking collectives: 40.3 us -> none  [per_device(): row_peak = lax.pmax(jnp.max(logits, axis=1), 'ch')]
    psum x1 -> x0, blocking collectives: 35.9 us -> none  [per_device(): lax.psum((jnp.sum(weights, axis=1), jnp.sum(weights * shifted, axis=1), j...]
    ppermute x16 -> x1, starting transfers between devices: 30.7 us -> 1.91 us  [per_device(): lax.ppermute(layer_input[TOK - (KCONV - 1):], 'ctx', [(i, i + 1) for i in...]
  transfers between devices with their start and end apart: 20 -> 2, of which waited for: 19 -> 0; matrix products, arithmetic and copies ran while one was open for 21% -> 4% of each run, Pallas kernels for 0% -> 70%
where the time goes in v1:
time: 182 us; the launch traced here: 181 us
  Pallas kernels  155 us (85%)
  between operations  14.1 us (8%)
  local copies, waits for them, and re-layouts  7.43 us (4%)
  starting transfers between devices  1.95 us (1%)
    pallas_call x1, Pallas kernels, mix(): pl.pallas_call(mix_kernel, out_shape=jax.ShapeDtypeStruct((TOK, D), BF16)...  61.9 us
    pallas_call x1, Pallas kernels, sum_projected(): pl.pallas_call(sum_projected_kernel, out_shape=(jax.ShapeDtypeStruct(part...  27 us
    pallas_call x1, Pallas kernels, score(): pl.pallas_call(score_kernel, out_shape=jax.ShapeDtypeStruct((TOK, 128), F...  16.6 us
    pallas_call x1, Pallas kernels, carry_in(): pl.pallas_call(carry_kernel, out_shape=jax.ShapeDtypeStruct((STATE * 8, 1...  15.8 us
    pallas_call x1, Pallas kernels, local_scan(): pl.pallas_call(scan_kernel, out_shape=(shape((FLAT, 128), F32), shape((FL...  13.3 us
    pallas_call x1, Pallas kernels, combine(): pl.pallas_call(combine_kernel, out_shape=jax.ShapeDtypeStruct((8, TOK), F...  10.9 us
    pallas_call x1, Pallas kernels, gated(): pl.pallas_call(gate_kernel, out_shape=jax.ShapeDtypeStruct((TOK, CH), BF1...  9.66 us
  transfers between devices with their start and end apart: 2, of which 0 were waited for; matrix products, arithmetic and copies ran while one was open for 4% of the time, Pallas kernels for 70%

profile of v1, /device:TPU:192, one launch (start us, length us, event | category | flops | bytes accessed | tf_op | source)
XLA Modules:
  0.0 181.2 jit_solution(604571687407482020)
XLA Ops:
  7.2 0.0 copy-start
  7.2 0.0 copy-start.2
  7.2 0.0 all-gather.2.cloned.1.call-start
  7.2 0.7 all-gather.2.cloned.1.call-update
  7.9 0.0 copy-start.3
  7.9 0.7 slice.44
  8.7 1.9 %collective-permute-start = (bf16[3,1024]{1,0:T(4,128)(2,1)S(1)}, bf16[3,1024]{1,0:T(4,128)(2,1)S(1)}, u32[]{:S(2)}, u32[]{:S(2)}) collective-permute-start(bf16[3,1024]{1,0:T(4,128)(2,1)S(1)} %slice.44), channel_id=1, source_target_pairs={{0,16},{16,32},{32,48},{48,64},{64,80},{80,96},{96,112},{112,128},... | collective-permute-start | bytes 18440 | tf_op jit(solution)/shard_map/ppermute | solution.py:603
  10.6 0.9 fusion.4
  11.5 1.5 reshape.10.decay
  12.9 1.5 broadcast_in_dim.18.targets
  14.4 0.0 collective-permute-done
  14.4 0.0 copy-done.2
  14.4 0.2 maximum_convert_fusion
  14.7 0.0 copy-done.3
  14.7 1.0 divide_convert_fusion.smoothed
  15.7 0.0 copy-done
  15.7 0.0 copy-start.1
  15.7 0.8 convolution_bitcast_fusion
  16.5 0.8 slice.93.part
  17.3 0.0 copy-done.1
  17.3 0.6 slice.62.bcpart
  17.9 27.0 %sum_projected.1 = (bf16[512,384]{1,0:T(8,128)(2,1)}, f32[32,384]{1,0:T(8,128)}) custom-call(bf16[512,384]{1,0:T(8,128)(2,1)} %slice.93.part, f32[32,384]{1,0:T(8,128)} %slice.62.bcpart), custom_call_target="tpu_custom_call" | custom-call | tf_op jit(solution)/shard_map/sum_projected/pallas_call | solution.py:122
  44.9 13.3 %local_scan.1 = (f32[3072,128]{1,0:T(8,128)}, f32[3072,128]{1,0:T(8,128)}, f32[128,128]{1,0:T(8,128)}, f32[8,128]{1,0:T(8,128)}) custom-call(bf16[512,384]{1,0:T(8,128)(2,1)} %get-tuple-element.9.proj, bf16[512,1024]{1,0:T(8,128)(2,1)} %step_w.1, f32[1,1024]{1,0:T(1,128)} %bitcast.17, f32[128,128]{1,0:T(8,128)} %reshape.10.decay, ...), custom_call_target="tpu_custom_call" | custom-call | tf_op jit(solution)/shard_map/local_scan/pallas_call | solution.py:188
  58.1 15.8 %carry_in.1.incoming = f32[128,128]{1,0:T(8,128)} custom-call(f32[128,128]{1,0:T(8,128)} %get-tuple-element.13.state, f32[8,128]{1,0:T(8,128)} %get-tuple-element.14.total, f32[128,128]{1,0:T(8,128)} %reshape.10.decay), custom_call_target="tpu_custom_call" | custom-call | tf_op jit(solution)/shard_map/carry_in/pallas_call | solution.py:277
  73.9 9.7 %gated.1.mixer = bf16[384,1024]{1,0:T(8,128)(2,1)} custom-call(f32[3072,128]{1,0:T(8,128)} %get-tuple-element.11.y, f32[3072,128]{1,0:T(8,128)} %get-tuple-element.12.e, f32[128,128]{1,0:T(8,128)} %carry_in.1.incoming, f32[128,128]{1,0:T(8,128)} %reshape.10.decay, f32[32,384]{1,0:T(8,128)} %get-tuple-element.10.bc, bf16[384,1024]{1,0:T(8,128)(2,1)} %copy-done.1, ...), custom_call_target="tpu_custom_call" | custom-call | tf_op jit(solution)/shard_map/gated/pallas_call | solution.py:327
  83.6 61.9 %mix.1.scaled = bf16[384,4096]{1,0:T(8,128)(2,1)} custom-call(bf16[384,1024]{1,0:T(8,128)(2,1)} %gated.1.mixer, bf16[1024,4096]{1,0:T(8,128)(2,1)} %weight.1, bf16[384,256]{1,0:T(8,128)(2,1)} %residual.1, f32[1,4096]{1,0:T(1,128)} %bitcast.11), custom_call_target="tpu_custom_call" | custom-call | tf_op jit(solution)/shard_map/mix/pallas_call | solution.py:458
  145.5 0.0 all-gather.2.cloned.1.call-done.head
  145.5 16.6 %score.1.packed = f32[384,128]{1,0:T(8,128)} custom-call(bf16[384,4096]{1,0:T(8,128)(2,1)} %mix.1.scaled, bf16[4096,2048]{1,0:T(8,128)(2,1)} %all-gather.2.cloned.1.call-done.head, f32[1,4096]{1,0:T(1,128)} %bitcast.12, s32[384,1]{1,0:T(8,128)} %broadcast_in_dim.18.targets), custom_call_target="tpu_custom_call" | custom-call | tf_op jit(solution)/shard_map/score/pallas_call | solution.py:528
  162.0 10.9 %combine.1 = f32[8,384]{1,0:T(8,128)} custom-call(f32[384,128]{1,0:T(8,128)} %score.1.packed), custom_call_target="tpu_custom_call" | custom-call | tf_op jit(solution)/shard_map/combine/pallas_call | solution.py:581
  172.9 1.4 slice_reduce_fusion
Async XLA Ops:
  7.2 8.5 %copy-start = (bf16[544,1024]{1,0:T(8,128)(2,1)S(1)}, bf16[544,1024]{1,0:T(8,128)(2,1)}, u32[]{:S(2)}) copy-start(bf16[544,1024]{1,0:T(8,128)(2,1)} %param.18) | copy-start | bytes 3342340
  7.2 7.2 %copy-start.2 = (bf16[384,1024]{1,0:T(8,128)(2,1)S(1)}, bf16[384,1024]{1,0:T(8,128)(2,1)}, u32[]{:S(2)}) copy-start(bf16[384,1024]{1,0:T(8,128)(2,1)} %param.14) | copy-start | bytes 2359300
  7.2 138.3 %all-gather.2.cloned.1.call-start = ((), (), s32[]{:S(2)}) async-start(), calls=%async_computation | async-start | bytes 17825792 | tf_op jit(solution)/shard_map/all_gather | solution.py:601
  7.9 6.7 %copy-start.3 = (f32[1024]{0:T(1024)S(1)}, f32[1024]{0:T(1024)}, u32[]{:S(2)}) copy-start(f32[1024]{0:T(1024)} %param.17) | copy-start | bytes 12292
  8.7 5.8 %collective-permute-start = (bf16[3,1024]{1,0:T(4,128)(2,1)S(1)}, bf16[3,1024]{1,0:T(4,128)(2,1)S(1)}, u32[]{:S(2)}, u32[]{:S(2)}) collective-permute-start(bf16[3,1024]{1,0:T(4,128)(2,1)S(1)} %slice.44), channel_id=1, source_target_pairs={{0,16},{16,32},{32,48},{48,64},{64,80},{80,96},{96,112},{112,128},... | collective-permute-start | bytes 18440 | tf_op jit(solution)/shard_map/ppermute | solution.py:603
  15.7 1.6 copy-start.1
Sparse Core Ops, SparseCore 0:
  9.8 96.8 all-gather.1

commit v2 on v0

v2 whole, which is shorter than its diff:
```python
import jax
import jax.numpy as jnp
from jax import lax
from jax.experimental import pallas as pl
from jax.experimental.pallas import tpu as pltpu
from jax.sharding import PartitionSpec as P

STATE = 16
RANK = 512
KCONV = 4
TOK = 384
CH = 1024
D = 4096
VOC = 2048
NCH = 16
NCTX = 16
NZ = 8
NT = 3
TC = TOK // NT
ROWS = RANK // NCH
NTB = TOK // 8
FLAT = NTB * 64
HALF = STATE * 4
NQ = 4
QR = TOK // NQ
BLK = D // NCH
HB = D // NCTX
HP = HB // 2
VT = 256
NVT = VOC // VT
MESH = pl.DeviceIdType.MESH
F32 = jnp.float32
BF16 = jnp.bfloat16
VM = pl.BlockSpec(memory_space=pltpu.VMEM)
HBM = pl.BlockSpec(memory_space=pl.ANY)
SLOT = (0, 8, 12, 14)


def remote(src, dst, send_sem, recv_sem, peer):
    return pltpu.make_async_remote_copy(
        src_ref=src, dst_ref=dst, send_sem=send_sem, recv_sem=recv_sem, device_id=peer, device_id_type=MESH
    )


def sigmoid_linear(operand):
    return operand / (1.0 + jnp.exp(-operand))


def cube_of(index):
    x, y = index // 4, lax.rem(index, 4)
    return [lax.rem(x + x // 2, 2), x // 2, lax.rem(y + y // 2, 2), y // 2]


def index_of(bits):
    def line(low, high):
        return high * 2 + lax.rem(high + low, 2)

    return line(bits[0], bits[1]) * 4 + line(bits[2], bits[3])


def kernel(
    xin, gate_in, select_in, stepw_in, outw_in, head_in, residual, conv_w, conv_b, step_b, decay_in, skip, gain, targets,
    out,
    xs, gs, sel, stepw, wv, head, halo, xpad, sm, sg, dflat, pb, bcp, recv, mine, proj, recvx, minex, bc, bb,
    dtf, uf, state, total, swap_s, got_s, got_e, send_s, send_e, zs, ze, hold, fin, into,
    mixer, acc, part, got, scaled, rms, tcol, stat, gstat,
    ld, hs, hr, hps, hpr, halos, halor, s1, r1, s2, r2, sx, rx, sy, ry, cs, cr, csz, crz, csf, crf, ms, mr, gsn, grv, es, er,
):
    ch = lax.axis_index("ch")
    ctx = lax.axis_index("ctx")
    z, c = ctx // 2, lax.rem(ctx, 2)
    pending = []

    def begin(copy):
        copy.start()
        pending.append(copy)
        return copy

    others = [lax.rem(ch + off, NCH) for off in range(1, NCH)]
    partner = {"ctx": z * 2 + 1 - c}
    after, before = lax.rem(ctx + 1, NCTX), lax.rem(ctx + NCTX - 1, NCTX)
    cross = jnp.where(c == 0, before, after)
    greeted = [{"ch": p} for p in others] + [partner, {"ctx": cross}]
    greeted += [{"ctx": lax.rem(z + d, NZ) * 2 + c} for d in range(1, NZ)]
    barrier = pltpu.get_barrier_semaphore()
    for peer in greeted:
        pl.semaphore_signal(barrier, inc=1, device_id=peer, device_id_type=MESH)

    own = pl.ds(pl.multiple_of(ctx * HB, HB), HB)
    local = [
        pltpu.make_async_copy(xin, xs, ld.at[0]),
        pltpu.make_async_copy(select_in, sel, ld.at[1]),
        pltpu.make_async_copy(stepw_in, stepw, ld.at[2]),
        pltpu.make_async_copy(gate_in, gs, ld.at[3]),
        pltpu.make_async_copy(head_in, head.at[own], ld.at[4]),
        pltpu.make_async_copy(outw_in, wv, ld.at[5]),
    ]
    for copy in local:
        copy.start()
    pl.semaphore_wait(barrier, len(greeted))

    @pl.when(ctx < NCTX - 1)
    def _():
        remote(xin.at[pl.ds(TOK - 16, 16)], halo, halos.at[0], halor.at[0], {"ctx": after}).start()

    right = {"ctx": lax.rem(z + 1, NZ) * 2 + c}
    left = {"ctx": lax.rem(z + NZ - 1, NZ) * 2 + c}

    def rows_of(zb, core, p):
        start = pl.multiple_of((zb * 2 + core) * HB + p * HP, HP)
        return head.at[pl.ds(start, HP)]

    def hop(way, k, p):
        zb = lax.rem(z + NZ - k, NZ) if way == 0 else lax.rem(z + k, NZ)
        where = rows_of(zb, c, p)
        src = head_in.at[pl.ds(p * HP, HP)] if k == 0 else where
        return remote(src, where, hs.at[way, k, p], hr.at[way, k, p], right if way == 0 else left)

    def arrival(way, k, p):
        zb = lax.rem(z + NZ - 1 - k, NZ) if way == 0 else lax.rem(z + 1 + k, NZ)
        where = rows_of(zb, c, p)
        return remote(where, where, hs.at[way, k, p], hr.at[way, k, p], right if way == 0 else left), where

    def valid(way, k, p):
        return k < 3 or (k == 3 and p == way)

    def pump(k, p):
        for way in range(2):
            if valid(way, k, p):
                got_it, where = arrival(way, k, p)
                got_it.wait_recv()
                if valid(way, k + 1, p):
                    begin(hop(way, k + 1, p))
                begin(remote(where, where, hps.at[way, k, p], hpr.at[way, k, p], partner))

    for p in range(2):
        for way in range(2):
            begin(hop(way, 0, p))
    mine_rows = head.at[own]
    begin(remote(head_in, mine_rows, hps.at[0, 3, 1], hpr.at[0, 3, 1], partner))

    for lt in range(8):
        lanes = slice(128 * lt, 128 * lt + 128)
        for h in range(2):
            dflat[pl.ds(lt + 64 * h, 8, stride=8), :] = decay_in[8 * h : 8 * h + 8, lanes]
    local[0].wait()
    for k in range(TOK // 32):
        xpad[8 + 32 * k : 40 + 32 * k, :] = xs[32 * k : 32 * k + 32, :].astype(F32)

    @pl.when(ctx > 0)
    def _():
        remote(xin.at[pl.ds(TOK - 16, 16)], halo, halos.at[0], halor.at[0], {"ctx": after}).wait_recv()
        xpad[0:8, :] = halo[...].astype(F32)[8:16, :]

    @pl.when(ctx == 0)
    def _():
        xpad[0:8, :] = jnp.zeros((8, CH), F32)

    local[1].wait()
    sends1 = {}
    for t in range(NT):
        for k in range(TC // 32):
            r0 = TC * t + 32 * k
            for half in range(2):
                lanes = slice(512 * half, 512 * half + 512)
                v = jnp.zeros((32, 512), F32) + conv_b[:, lanes]
                for offset in range(KCONV):
                    v = v + conv_w[offset : offset + 1, lanes] * xpad[r0 + 5 + offset : r0 + 37 + offset, lanes]
                sm[r0 : r0 + 32, lanes] = sigmoid_linear(v).astype(BF16)
        product = lax.dot_general(
            sel[...], sm[TC * t : TC * t + TC, :], (((1,), (1,)), ((), ())), preferred_element_type=F32
        )
        pb[t] = product[:RANK].astype(BF16)
        bcp[t] = product[RANK:]
        for k, p in enumerate(others):
            rows = pl.ds(pl.multiple_of(p * ROWS, ROWS), ROWS)
            sends1[t, k] = begin(remote(pb.at[t, rows], recv.at[t, k], s1.at[t, k], r1.at[t, k], {"ch": p}))
        for k in range(4):
            @pl.when(ch != 5 * k)
            def _():
                tile(t, k, ch, bcp, recvx, sx, rx).start()

    local[3].wait()
    for k in range(TOK // 32):
        sg[32 * k : 32 * k + 32, :] = sigmoid_linear(gs[32 * k : 32 * k + 32, :].astype(F32))

    myrows = pl.ds(pl.multiple_of(ch * ROWS, ROWS), ROWS)
    sends2 = {}
    for t in range(NT):
        for k in range(NCH - 1):
            sends1[t, k].wait_recv()
        summed = pb[t, myrows].astype(F32)
        for k in range(NCH - 1):
            summed = summed + recv[t, k].astype(F32)
        mine[t] = summed.astype(BF16)
        for k, p in enumerate(others):
            sends2[t, k] = begin(remote(mine.at[t], proj.at[t, myrows], s2.at[t, k], r2.at[t, k], {"ch": p}))
        proj[t, myrows] = mine[t]
        for k in range(4):
            @pl.when(ch == 5 * k)
            def _():
                sumx = bcp[t, 8 * k : 8 * k + 8]
                for j in range(NCH - 1):
                    remote(minex.at[t], recvx.at[t, j], sx.at[t, 0], rx.at[t, j], {"ch": others[0]}).wait_recv()
                    sumx = sumx + recvx[t, j]
                minex[t] = sumx
                for j in range(NCH - 1):
                    remote(
                        minex.at[t], bc.at[t, pl.ds(8 * k, 8)], sy.at[t, j], ry.at[t, k], {"ch": others[j]}
                    ).start()
                bc[t, 8 * k : 8 * k + 8] = minex[t]

    pump(0, 0)

    local[2].wait()
    rates = [-jnp.exp(dflat[8 * n : 8 * n + 8, :]) for n in range(STATE)]
    carry = (jnp.zeros((8, 128), F32),) * (STATE + 1)
    for t in range(NT):
        for k in range(NCH - 1):
            sends2[t, k].wait_recv()
        for k in range(4):
            @pl.when(ch != 5 * k)
            def _():
                remote(minex.at[t], bc.at[t, pl.ds(8 * k, 8)], sy.at[t, 0], ry.at[t, k], {"ch": 5 * k}).wait_recv()

        turned = jnp.transpose(bc[t])
        for n in range(2 * STATE):
            bb[n, TC * t : TC * t + TC, :] = jnp.broadcast_to(turned[:, n : n + 1], (TC, 128))
        raw = lax.dot_general(proj[t], stepw[...], (((0,), (0,)), ((), ())), preferred_element_type=F32)
        v = raw + step_b[...]
        dt = jnp.maximum(v, 0.0) + jnp.log1p(jnp.exp(-jnp.abs(v)))
        u = dt * sm[TC * t : TC * t + TC, :].astype(F32)
        for b in range(TC // 8):
            for lt in range(8):
                start = (TC // 8 * t + b) * 64 + lt * 8
                dtf[start : start + 8, :] = dt[8 * b : 8 * b + 8, 128 * lt : 128 * lt + 128]
                uf[start : start + 8, :] = u[8 * b : 8 * b + 8, 128 * lt : 128 * lt + 128]

        def step(tb, held):
            s, elapsed = list(held[:STATE]), held[STATE]
            for r in range(8):
                rows = pl.ds(tb * 64 + r, 8, stride=8)
                dt = dtf[rows, :]
                u = uf[rows, :]
                splat = pl.ds(tb * 8 + r, 8, stride=0)
                y = None
                for n in range(STATE):
                    s[n] = jnp.exp(dt * rates[n]) * s[n] + u * bb[n, splat, :]
                    term = s[n] * bb[STATE + n, splat, :]
                    y = term if y is None else y + term
                elapsed = elapsed + dt
                uf[rows, :] = y
                dtf[rows, :] = elapsed
            return (*s, elapsed)

        carry = lax.fori_loop(TC // 8 * t, TC // 8 * (t + 1), step, carry)
        if t == 1:
            pump(0, 1)
    for n in range(STATE):
        state[8 * n : 8 * n + 8, :] = carry[n]
    total[...] = carry[STATE]

    half = pl.ds(pl.multiple_of(c * HALF, HALF), HALF)
    other = pl.ds(pl.multiple_of((1 - c) * HALF, HALF), HALF)
    swap_s[...] = state[other, :]
    a = begin(remote(swap_s, got_s, cs.at[0], cr.at[0], partner))
    b = begin(remote(total, got_e, cs.at[1], cr.at[1], partner))
    rate = -jnp.exp(dflat[half, :])

    def through(elapsed):
        return jnp.exp(rate * jnp.tile(elapsed, (HALF // 8, 1)))

    a.wait_recv()
    b.wait_recv()
    own_s, own_e, oth_s, oth_e = state[half, :], total[...], got_s[...], got_e[...]
    low = c == 0
    t0, t1 = jnp.where(low, own_s, oth_s), jnp.where(low, oth_s, own_s)
    e0, e1 = jnp.where(low, own_e, oth_e), jnp.where(low, oth_e, own_e)
    send_s[...] = (through(e1) * t0 + t1).astype(send_s.dtype)
    send_e[...] = e0 + e1

    def pair(d, sign):
        peer = {"ctx": (z + sign * d) * 2 + c}
        return (
            remote(send_s, zs.at[d - 1], csz.at[0, d - 1], crz.at[0, d - 1], peer),
            remote(send_e, ze.at[d - 1], csz.at[1, d - 1], crz.at[1, d - 1], peer),
        )

    for d in range(1, NZ):
        @pl.when(z + d < NZ)
        def _():
            for copy in pair(d, 1):
                copy.start()

    pump(1, 0)
    hold[...] = jnp.zeros_like(hold)
    for d in range(NZ - 1, 0, -1):
        @pl.when(z >= d)
        def _():
            for copy in pair(d, -1):
                copy.wait_recv()
            hold[...] = through(ze[d - 1]) * hold[...] + zs[d - 1].astype(F32)

    into0 = hold[...]
    into1 = through(e0) * into0 + t0
    fin[...] = jnp.where(low, into1, into0)
    into[half, :] = jnp.where(low, into0, into1)
    f = begin(remote(fin, into.at[half], csf.at[0], crf.at[0], partner))
    f.wait_recv()

    came = [into[8 * n : 8 * n + 8, :] for n in range(STATE)]

    def fix(tb, _):
        for r in range(8):
            rows = pl.ds(tb * 64 + r, 8, stride=8)
            elapsed = dtf[rows, :]
            y = uf[rows, :]
            splat = pl.ds(tb * 8 + r, 8, stride=0)
            for n in range(STATE):
                y = y + jnp.exp(elapsed * rates[n]) * came[n] * bb[STATE + n, splat, :]
            uf[rows, :] = y
        return 0

    lax.fori_loop(0, NTB, fix, 0)
    for k in range(TOK // 16):
        rows = slice(16 * k, 16 * k + 16)
        for lt in range(8):
            lanes = slice(128 * lt, 128 * lt + 128)
            start = (2 * k) * 64 + lt * 8
            scanned = jnp.concatenate([uf[start : start + 8, :], uf[start + 64 : start + 72, :]], axis=0)
            value = scanned + skip[:, lanes] * sm[rows, lanes].astype(F32)
            mixer[rows, lanes] = (value * sg[rows, lanes]).astype(BF16)
    pump(1, 1)

    bits = cube_of(ch)

    def block(r):
        return index_of([lax.rem(bits[d] + ((r >> d) & 1), 2) for d in range(4)])

    def lanes_of(r):
        return pl.ds(pl.multiple_of(block(r) * BLK, BLK), BLK)

    peers = [{"ch": block(1 << d)} for d in range(4)]

    def rows(q):
        return pl.ds(QR * q, QR)

    def dim(q, s):
        return (q + s) % 4

    def kept(q, s):
        return [r for r in range(16) if all(not (r >> dim(q, i)) & 1 for i in range(s))]

    def slot(q, s, r):
        return SLOT[s] + kept(q, s + 1).index(r)

    def send(q, s, r):
        d = dim(q, s)
        k = slot(q, s, r ^ (1 << d))
        begin(remote(part.at[r, rows(q)], got.at[k, rows(q)], ms.at[r, q], mr.at[k, q], peers[d]))

    def take(q, s, r):
        k = slot(q, s, r)
        remote(part.at[r, rows(q)], got.at[k, rows(q)], ms.at[r, q], mr.at[k, q], peers[dim(q, s)]).wait_recv()
        return got[k, rows(q)].astype(F32)

    local[5].wait()
    for r in [15, 14, 13, 11, 7, 12, 10, 9, 6, 5, 3, 8, 4, 2, 1, 0]:
        product = jnp.dot(mixer[...], wv[:, lanes_of(r)], preferred_element_type=F32)
        acc[r] = product
        part[r] = product.astype(BF16)
        for q in range(NQ):
            if (r >> dim(q, 0)) & 1:
                send(q, 0, r)
    pump(2, 0)
    for s in range(3):
        for q in range(NQ):
            left_over = kept(q, s + 1)
            d = dim(q, s + 1)
            for r in [r for r in left_over if (r >> d) & 1] + [r for r in left_over if not (r >> d) & 1]:
                value = acc[r, rows(q)] + take(q, s, r)
                if (r >> d) & 1:
                    part[r, rows(q)] = value.astype(BF16)
                    send(q, s + 1, r)
                else:
                    acc[r, rows(q)] = value
        if s == 1:
            pump(2, 1)

    def give(q, s, r):
        d = dim(q, s)
        where = scaled.at[rows(q), lanes_of(r)]
        begin(remote(where, where, gsn.at[q, s, r], grv.at[q, s, r ^ (1 << d)], peers[d]))

    def spread(q, s):
        held = [0]
        for i in range(s):
            held = held + [r ^ (1 << dim(q, i)) for r in held]
        return held

    for q in range(NQ):
        hidden = residual[rows(q), :].astype(F32) + (acc[0, rows(q)] + take(q, 3, 0))
        scaled[rows(q), lanes_of(0)] = (hidden * gain[:, lanes_of(0)]).astype(BF16)
        give(q, 0, 0)
    for s in range(4):
        for q in range(NQ):
            for r in spread(q, s):
                r = r ^ (1 << dim(q, s))
                where = scaled.at[rows(q), lanes_of(r)]
                remote(where, where, gsn.at[q, s, r], grv.at[q, s, r], peers[dim(q, s)]).wait_recv()
            if s < 3:
                for r in spread(q, s + 1):
                    give(q, s + 1, r)
        if s == 1:
            for p in range(2):
                pump(3, p)

    local[4].wait()
    for k in range(4):
        for p in range(2):
            for way in range(2):
                if valid(way, k, p):
                    where = head.at[pl.ds(0, HP)]
                    remote(where, where, hps.at[way, k, p], hpr.at[way, k, p], partner).wait_recv()
    remote(head_in, mine_rows, hps.at[0, 3, 1], hpr.at[0, 3, 1], partner).wait_recv()

    def square(k, held):
        where = pl.ds(pl.multiple_of(k * BLK, BLK), BLK)
        h = scaled[:, where].astype(F32) / gain[:, where]
        acc[8] += h * h
        return held

    acc[8] = jnp.zeros((TOK, BLK), F32)
    lax.fori_loop(0, NCH, square, 0)
    rms[...] = lax.rsqrt(jnp.sum(acc[8], axis=1, keepdims=True) * (1.0 / D) + 1e-06)

    def logit(j, held):
        where = pl.ds(pl.multiple_of(j * VT, VT), VT)
        acc[j] = jnp.dot(scaled[...], head[:, where], preferred_element_type=F32) * rms[...]
        return held

    lax.fori_loop(0, NVT, logit, 0)
    tcol[...] = jnp.transpose(jnp.broadcast_to((targets[...] - ch * VOC).astype(F32), (128, TOK)))
    lane = lax.broadcasted_iota(jnp.int32, (32, VT), 1).astype(F32)
    place = lax.broadcasted_iota(jnp.int32, (32, 128), 1)

    def tally(k, held):
        here = pl.ds(pl.multiple_of(k * 32, 32), 32)
        values = [acc[j, here] for j in range(NVT)]
        peak = values[0]
        for v in values[1:]:
            peak = jnp.maximum(peak, v)
        peak = jnp.max(peak, axis=1, keepdims=True)
        want = tcol[here, :][:, 0:1]
        sums = [jnp.zeros((32, VT), F32) for _ in range(4)]
        for j, v in enumerate(values):
            shifted = v - peak
            w = jnp.exp(shifted)
            ws = w * shifted
            sums[0] = sums[0] + w
            sums[1] = sums[1] + ws
            sums[2] = sums[2] + ws * shifted
            sums[3] = sums[3] + jnp.where(lane + float(j * VT) == want, v, 0.0)
        cols = [peak] + [jnp.sum(v, axis=1, keepdims=True) for v in sums]
        packed = jnp.zeros((32, 128), F32)
        for i, v in enumerate(cols):
            packed = jnp.where(place == i, v, packed)
        tcol[here, :] = packed
        return held

    lax.fori_loop(0, TOK // 32, tally, 0)

    stat[...] = jnp.transpose(tcol[...])[:8, :]
    sends3 = [begin(remote(stat, gstat.at[k], es.at[k], er.at[k], {"ch": p})) for k, p in enumerate(others)]
    for copy in sends3:
        copy.wait_recv()
    parts = [stat[...]] + [gstat[k] for k in range(NCH - 1)]
    peak = parts[0][0:1, :]
    for v in parts[1:]:
        peak = jnp.maximum(peak, v[0:1, :])
    sum0 = sum1 = sum2 = picked = jnp.zeros((1, TOK), F32)
    for v in parts:
        d = v[0:1, :] - peak
        w = jnp.exp(d)
        wd = w * d
        sum0 = sum0 + w * v[1:2, :]
        sum1 = sum1 + (w * v[2:3, :] + wd * v[1:2, :])
        sum2 = sum2 + (w * v[3:4, :] + 2.0 * wd * v[2:3, :] + wd * d * v[1:2, :])
        picked = picked + v[4:5, :]
    log_total = jnp.log(sum0)
    ratio = sum1 / sum0
    out[0:1, :] = picked - peak - log_total
    out[1:2, :] = ratio - log_total
    out[2:3, :] = sum2 / sum0 - ratio * ratio
    out[3:8, :] = jnp.zeros((5, TOK), F32)

    for copy in pending:
        copy.wait_send()

    @pl.when(ctx < NCTX - 1)
    def _():
        remote(xin.at[pl.ds(TOK - 16, 16)], halo, halos.at[0], halor.at[0], {"ctx": after}).wait_send()

    for d in range(1, NZ):
        @pl.when(z + d < NZ)
        def _():
            for copy in pair(d, 1):
                copy.wait_send()
    for t in range(NT):
        for k in range(4):
            @pl.when(ch != 5 * k)
            def _():
                tile(t, k, ch, bcp, recvx, sx, rx).wait_send()

            @pl.when(ch == 5 * k)
            def _():
                for j in range(NCH - 1):
                    remote(
                        minex.at[t], bc.at[t, pl.ds(8 * k, 8)], sy.at[t, j], ry.at[t, k], {"ch": others[j]}
                    ).wait_send()


def tile(t, k, ch, bcp, recvx, sx, rx):
    where = lax.rem(ch - 5 * k + 2 * NCH, NCH) - 1
    return remote(bcp.at[t, pl.ds(8 * k, 8)], recvx.at[t, where], sx.at[t, k], rx.at[t, where], {"ch": 5 * k})


def per_device(
    layer_input, gate_input, conv_weight, conv_bias, select_weight, step_weight, step_bias, decay_log,
    skip_gain, out_weight, residual, norm_gain, head_weight, targets,
):
    n = NCH - 1
    dma = pltpu.SemaphoreType.DMA
    v = pltpu.VMEM
    result = pl.pallas_call(
        kernel,
        out_shape=jax.ShapeDtypeStruct((8, TOK), F32),
        in_specs=[HBM] * 6 + [VM] * 8,
        out_specs=VM,
        scratch_shapes=[
            v((TOK, CH), BF16), v((TOK, CH), BF16), v((RANK + 2 * STATE, CH), BF16), v((RANK, CH), BF16),
            v((CH, D), BF16), v((D, VOC), BF16), v((16, CH), BF16), v((TOK + 8, CH), F32), v((TOK, CH), BF16),
            v((TOK, CH), F32), v((STATE * 8, 128), F32),
            v((NT, RANK, TC), BF16), v((NT, 2 * STATE, TC), F32), v((NT, n, ROWS, TC), BF16), v((NT, ROWS, TC), BF16),
            v((NT, RANK, TC), BF16), v((NT, n, 8, TC), F32), v((NT, 8, TC), F32), v((NT, 2 * STATE, TC), F32),
            v((2 * STATE, TOK, 128), F32),
            v((FLAT, 128), F32), v((FLAT, 128), F32), v((STATE * 8, 128), F32), v((8, 128), F32),
            v((HALF, 128), F32), v((HALF, 128), F32), v((8, 128), F32),
            v((HALF, 128), BF16), v((8, 128), F32), v((NZ - 1, HALF, 128), BF16), v((NZ - 1, 8, 128), F32),
            v((HALF, 128), F32), v((HALF, 128), F32), v((STATE * 8, 128), F32),
            v((TOK, CH), BF16), v((NCH, TOK, BLK), F32), v((NCH, TOK, BLK), BF16), v((15, TOK, BLK), BF16),
            v((TOK, D), BF16), v((TOK, 1), F32), v((TOK, 128), F32), v((8, TOK), F32), v((n, 8, TOK), F32),
            dma((6,)), dma((2, 4, 2)), dma((2, 4, 2)), dma((2, 4, 2)), dma((2, 4, 2)), dma((1,)), dma((1,)),
            dma((NT, n)), dma((NT, n)), dma((NT, n)), dma((NT, n)),
            dma((NT, 4)), dma((NT, n)), dma((NT, n)), dma((NT, 4)),
            dma((2,)), dma((2,)), dma((2, NZ - 1)), dma((2, NZ - 1)), dma((1,)), dma((1,)),
            dma((NCH, NQ)), dma((15, NQ)), dma((NQ, 4, NCH)), dma((NQ, 4, NCH)), dma((n,)), dma((n,)),
        ],
        compiler_params=pltpu.CompilerParams(
            vmem_limit_bytes=67043328, collective_id=0, has_side_effects=True
        ),
        name="score_window",
    )(
        layer_input, gate_input, select_weight, step_weight, out_weight, head_weight, residual, conv_weight,
        conv_bias[None, :], step_bias[None, :], decay_log, skip_gain[None, :], norm_gain[None, :], targets[None, :],
    )
    return result[0], result[1], result[2]


def solution(mesh):
    in_specs = (
        P("ctx", "ch"), P("ctx", "ch"), P(None, "ch"), P("ch"), P(None, "ch"), P(None, "ch"), P("ch"),
        P(None, "ch"), P("ch"), P("ch", None), P("ctx", "ch"), P(), P("ctx", "ch"), P("ctx"),
    )
    return jax.shard_map(
        per_device, mesh=mesh, in_specs=in_specs, out_specs=(P("ctx"), P("ctx"), P("ctx")), check_vma=False
    )
```

time: 694 us -> 147 us (0.21); the launches traced: 683 us -> 147 us
  waiting for transfers between devices: 392 us -> 0 us
  Pallas kernels: 0 us -> 144 us
  local copies, waits for them, and re-layouts: 95.7 us -> 2.67 us
  blocking collectives: 76.2 us -> 0 us
  other arithmetic: 45 us -> 0 us
  starting transfers between devices: 31.1 us -> 0 us
  matrix products: 25.1 us -> 0 us
  between operations: 14.2 us -> 0.64 us
    psum x2 -> x0, waiting for transfers between devices: 237 us -> none  [the longest x1 142 us: per_device(): lax.psum(jnp.dot(mixer_input, out_weight, preferred_element_type=jnp.floa...]
    pallas_call x0 -> x1, Pallas kernels: none -> 144 us  [per_device(): pl.pallas_call(kernel, out_shape=jax.ShapeDtypeStruct((8, TOK), F32), in_...]
    all_gather x2 -> x0, waiting for transfers between devices: 90.3 us -> none  [the longest x1 90.3 us: per_device(): lax.all_gather(head_weight, 'ctx', axis=0, tiled=True)]
    slice x53 -> x1, local copies, waits for them, and re-layouts: 67.3 us -> 1.42 us  [per_device(): return (result[0], result[1], result[2])]
    ppermute x16 -> x0, waiting for transfers between devices: 63.9 us -> none  [from_behind(): return lax.ppermute(shard, axis, pairs)]
    pmax x1 -> x0, blocking collectives: 40.3 us -> none  [per_device(): row_peak = lax.pmax(jnp.max(logits, axis=1), 'ch')]
    psum x1 -> x0, blocking collectives: 35.9 us -> none  [per_device(): lax.psum((jnp.sum(weights, axis=1), jnp.sum(weights * shifted, axis=1), j...]
    ppermute x16 -> x0, starting transfers between devices: 30.7 us -> none  [from_behind(): return lax.ppermute(shard, axis, pairs)]
  transfers between devices with their start and end apart: 20 -> 0, of which waited for: 19 -> 0; matrix products, arithmetic and copies ran while one was open for 21% -> 0% of each run, Pallas kernels for 0% -> 0%
where the time goes in v2:
time: 147 us
  Pallas kernels  144 us (98%)
  local copies, waits for them, and re-layouts  2.67 us (2%)
    pallas_call x1, Pallas kernels, per_device(): pl.pallas_call(kernel, out_shape=jax.ShapeDtypeStruct((8, TOK), F32), in_...  144 us

profile of v2, /device:TPU:192, one launch (start us, length us, event | category | flops | bytes accessed | tf_op | source)
XLA Modules:
  0.0 147.2 jit_solution(2939901094835697899)
XLA Ops:
  0.6 1.2 broadcast_in_dim.19.targets
  1.9 143.9 %score_window.1 = f32[8,384]{1,0:T(8,128)} custom-call(bf16[384,1024]{1,0:T(8,128)(2,1)} %xin.1, bf16[384,1024]{1,0:T(8,128)(2,1)} %gate_in.1, bf16[544,1024]{1,0:T(8,128)(2,1)} %select_in.1, bf16[512,1024]{1,0:T(8,128)(2,1)} %stepw_in.1, bf16[1024,4096]{1,0:T(8,128)(2,1)} %outw_in.1, bf16[256,2048]{1,0:T(8,128)(2,1)} %head_in.1, bf16[384,256]{1,0:T(8,128)(2,1)} %residual.1, ...), custom_call_target="tpu_custom_call" | custom-call | tf_op jit(solution)/shard_map/score_window/pallas_call | solution.py:535
  145.8 1.4 slice_reduce_fusion

commit v3 on v2

--- a/solution.py
+++ b/solution.py
@@ -21,7 +21,9 @@
 NTB = TOK // 8
 FLAT = NTB * 64
 HALF = STATE * 4
-NQ = 4
+NK = 2
+TK = TOK // NK
+NQ = 4 * NK
 QR = TOK // NQ
 BLK = D // NCH
 HB = D // NCTX
@@ -124,14 +126,22 @@
     def valid(way, k, p):
         return k < 3 or (k == 3 and p == way)
 
-    def pump(k, p):
+    def relay(k, p):
         for way in range(2):
             if valid(way, k, p):
-                got_it, where = arrival(way, k, p)
-                got_it.wait_recv()
+                arrival(way, k, p)[0].wait_recv()
                 if valid(way, k + 1, p):
                     begin(hop(way, k + 1, p))
+
+    def share(k, p):
+        for way in range(2):
+            if valid(way, k, p):
+                where = arrival(way, k, p)[1]
                 begin(remote(where, where, hps.at[way, k, p], hpr.at[way, k, p], partner))
+
+    def pump(k, p):
+        relay(k, p)
+        share(k, p)
 
     for p in range(2):
         for way in range(2):
@@ -254,8 +264,6 @@
             return (*s, elapsed)
 
         carry = lax.fori_loop(TC // 8 * t, TC // 8 * (t + 1), step, carry)
-        if t == 1:
-            pump(0, 1)
     for n in range(STATE):
         state[8 * n : 8 * n + 8, :] = carry[n]
     total[...] = carry[STATE]
@@ -292,7 +300,7 @@
             for copy in pair(d, 1):
                 copy.start()
 
-    pump(1, 0)
+    relay(0, 1)
     hold[...] = jnp.zeros_like(hold)
     for d in range(NZ - 1, 0, -1):
         @pl.when(z >= d)
@@ -307,6 +315,9 @@
     into[half, :] = jnp.where(low, into0, into1)
     f = begin(remote(fin, into.at[half], csf.at[0], crf.at[0], partner))
     f.wait_recv()
+    relay(1, 0)
+    share(0, 1)
+    share(1, 0)
 
     came = [into[8 * n : 8 * n + 8, :] for n in range(STATE)]
 
@@ -321,16 +332,16 @@
             uf[rows, :] = y
         return 0
 
-    lax.fori_loop(0, NTB, fix, 0)
-    for k in range(TOK // 16):
-        rows = slice(16 * k, 16 * k + 16)
-        for lt in range(8):
-            lanes = slice(128 * lt, 128 * lt + 128)
-            start = (2 * k) * 64 + lt * 8
-            scanned = jnp.concatenate([uf[start : start + 8, :], uf[start + 64 : start + 72, :]], axis=0)
-            value = scanned + skip[:, lanes] * sm[rows, lanes].astype(F32)
-            mixer[rows, lanes] = (value * sg[rows, lanes]).astype(BF16)
-    pump(1, 1)
+    def gate_chunk(ck):
+        lax.fori_loop(NTB // NK * ck, NTB // NK * (ck + 1), fix, 0)
+        for k in range(TK // 16 * ck, TK // 16 * (ck + 1)):
+            rows = slice(16 * k, 16 * k + 16)
+            for lt in range(8):
+                lanes = slice(128 * lt, 128 * lt + 128)
+                start = (2 * k) * 64 + lt * 8
+                scanned = jnp.concatenate([uf[start : start + 8, :], uf[start + 64 : start + 72, :]], axis=0)
+                value = scanned + skip[:, lanes] * sm[rows, lanes].astype(F32)
+                mixer[rows, lanes] = (value * sg[rows, lanes]).astype(BF16)
 
     bits = cube_of(ch)
 
@@ -364,17 +375,21 @@
         remote(part.at[r, rows(q)], got.at[k, rows(q)], ms.at[r, q], mr.at[k, q], peers[dim(q, s)]).wait_recv()
         return got[k, rows(q)].astype(F32)
 
-    local[5].wait()
-    for r in [15, 14, 13, 11, 7, 12, 10, 9, 6, 5, 3, 8, 4, 2, 1, 0]:
-        product = jnp.dot(mixer[...], wv[:, lanes_of(r)], preferred_element_type=F32)
-        acc[r] = product
-        part[r] = product.astype(BF16)
-        for q in range(NQ):
-            if (r >> dim(q, 0)) & 1:
-                send(q, 0, r)
-    pump(2, 0)
-    for s in range(3):
-        for q in range(NQ):
+    def groups(ck):
+        return range(4 * ck, 4 * ck + 4)
+
+    def multiply(ck):
+        here = slice(TK * ck, TK * ck + TK)
+        for r in [15, 14, 13, 11, 7, 12, 10, 9, 6, 5, 3, 8, 4, 2, 1, 0]:
+            product = jnp.dot(mixer[here, :], wv[:, lanes_of(r)], preferred_element_type=F32)
+            acc[r, here] = product
+            part[r, here] = product.astype(BF16)
+            for q in groups(ck):
+                if (r >> dim(q, 0)) & 1:
+                    send(q, 0, r)
+
+    def fold(ck, s):
+        for q in groups(ck):
             left_over = kept(q, s + 1)
             d = dim(q, s + 1)
             for r in [r for r in left_over if (r >> d) & 1] + [r for r in left_over if not (r >> d) & 1]:
@@ -384,13 +399,6 @@
                     send(q, s + 1, r)
                 else:
                     acc[r, rows(q)] = value
-        if s == 1:
-            pump(2, 1)
-
-    def give(q, s, r):
-        d = dim(q, s)
-        where = scaled.at[rows(q), lanes_of(r)]
-        begin(remote(where, where, gsn.at[q, s, r], grv.at[q, s, r ^ (1 << d)], peers[d]))
 
     def spread(q, s):
         held = [0]
@@ -398,22 +406,72 @@
             held = held + [r ^ (1 << dim(q, i)) for r in held]
         return held
 
-    for q in range(NQ):
-        hidden = residual[rows(q), :].astype(F32) + (acc[0, rows(q)] + take(q, 3, 0))
-        scaled[rows(q), lanes_of(0)] = (hidden * gain[:, lanes_of(0)]).astype(BF16)
-        give(q, 0, 0)
-    for s in range(4):
-        for q in range(NQ):
+    def give(q, s, r):
+        k = (1 << s) - 1 + spread(q, s).index(r)
+        where = scaled.at[rows(q), lanes_of(r)]
+        begin(remote(where, where, gsn.at[q, k], grv.at[q, k], peers[dim(q, s)]))
+
+    def finish(ck):
+        for q in groups(ck):
+            hidden = residual[rows(q), :].astype(F32) + (acc[0, rows(q)] + take(q, 3, 0))
+            scaled[rows(q), lanes_of(0)] = (hidden * gain[:, lanes_of(0)]).astype(BF16)
+            give(q, 0, 0)
+
+    def widen(ck, s):
+        for q in groups(ck):
             for r in spread(q, s):
-                r = r ^ (1 << dim(q, s))
-                where = scaled.at[rows(q), lanes_of(r)]
-                remote(where, where, gsn.at[q, s, r], grv.at[q, s, r], peers[dim(q, s)]).wait_recv()
+                k = (1 << s) - 1 + spread(q, s).index(r)
+                where = scaled.at[rows(q), lanes_of(r ^ (1 << dim(q, s)))]
+                remote(where, where, gsn.at[q, k], grv.at[q, k], peers[dim(q, s)]).wait_recv()
             if s < 3:
                 for r in spread(q, s + 1):
                     give(q, s + 1, r)
-        if s == 1:
-            for p in range(2):
-                pump(3, p)
+
+    def logits(ck):
+        here = slice(TK * ck, TK * ck + TK)
+
+        def square(k, held):
+            where = pl.ds(pl.multiple_of(k * BLK, BLK), BLK)
+            h = scaled[here, where].astype(F32) / gain[:, where]
+            acc[8, here] += h * h
+            return held
+
+        acc[8, here] = jnp.zeros((TK, BLK), F32)
+        lax.fori_loop(0, NCH, square, 0)
+        rms[here, :] = lax.rsqrt(jnp.sum(acc[8, here], axis=1, keepdims=True) * (1.0 / D) + 1e-06)
+
+        def logit(j, held):
+            where = pl.ds(pl.multiple_of(j * VT, VT), VT)
+            acc[j, here] = jnp.dot(scaled[here, :], head[:, where], preferred_element_type=F32) * rms[here, :]
+            return held
+
+        lax.fori_loop(0, NVT, logit, 0)
+
+    gate_chunk(0)
+    local[5].wait()
+    multiply(0)
+    gate_chunk(1)
+    pump(1, 1)
+    fold(0, 0)
+    multiply(1)
+    fold(0, 1)
+    fold(1, 0)
+    pump(2, 0)
+    fold(0, 2)
+    fold(1, 1)
+    finish(0)
+    fold(1, 2)
+    pump(2, 1)
+    widen(0, 0)
+    finish(1)
+    widen(0, 1)
+    widen(1, 0)
+    widen(0, 2)
+    widen(1, 1)
+    widen(1, 2)
+    widen(0, 3)
+    for p in range(2):
+        pump(3, p)
 
     local[4].wait()
     for k in range(4):
@@ -424,22 +482,9 @@
                     remote(where, where, hps.at[way, k, p], hpr.at[way, k, p], partner).wait_recv()
     remote(head_in, mine_rows, hps.at[0, 3, 1], hpr.at[0, 3, 1], partner).wait_recv()
 
-    def square(k, held):
-        where = pl.ds(pl.multiple_of(k * BLK, BLK), BLK)
-        h = scaled[:, where].astype(F32) / gain[:, where]
-        acc[8] += h * h
-        return held
-
-    acc[8] = jnp.zeros((TOK, BLK), F32)
-    lax.fori_loop(0, NCH, square, 0)
-    rms[...] = lax.rsqrt(jnp.sum(acc[8], axis=1, keepdims=True) * (1.0 / D) + 1e-06)
-
-    def logit(j, held):
-        where = pl.ds(pl.multiple_of(j * VT, VT), VT)
-        acc[j] = jnp.dot(scaled[...], head[:, where], preferred_element_type=F32) * rms[...]
-        return held
-
-    lax.fori_loop(0, NVT, logit, 0)
+    logits(0)
+    widen(1, 3)
+    logits(1)
     tcol[...] = jnp.transpose(jnp.broadcast_to((targets[...] - ch * VOC).astype(F32), (128, TOK)))
     lane = lax.broadcasted_iota(jnp.int32, (32, VT), 1).astype(F32)
     place = lax.broadcasted_iota(jnp.int32, (32, 128), 1)
@@ -554,7 +599,7 @@
             dma((NT, n)), dma((NT, n)), dma((NT, n)), dma((NT, n)),
             dma((NT, 4)), dma((NT, n)), dma((NT, n)), dma((NT, 4)),
             dma((2,)), dma((2,)), dma((2, NZ - 1)), dma((2, NZ - 1)), dma((1,)), dma((1,)),
-            dma((NCH, NQ)), dma((15, NQ)), dma((NQ, 4, NCH)), dma((NQ, 4, NCH)), dma((n,)), dma((n,)),
+            dma((NCH, NQ)), dma((15, NQ)), dma((NQ, 15)), dma((NQ, 15)), dma((n,)), dma((n,)),
         ],
         compiler_params=pltpu.CompilerParams(
             vmem_limit_bytes=67043328, collective_id=0, has_side_effects=True

time: 147 us -> 133 us (0.905)
  the two profiles are of different devices: /device:TPU:192 before, /device:TPU:1 now
where the time goes in v3:
time: 133 us
  Pallas kernels  130 us (98%)
  local copies, waits for them, and re-layouts  2.67 us (2%)
    pallas_call x1, Pallas kernels, per_device(): pl.pallas_call(kernel, out_shape=jax.ShapeDtypeStruct((8, TOK), F32), in_...  130 us

profile of v3, /device:TPU:1, one launch (start us, length us, event | category | flops | bytes accessed | tf_op | source)
XLA Modules:
  0.0 133.2 jit_solution(1655515636795996914)
XLA Ops:
  0.6 1.2 broadcast_in_dim.19.targets
  1.9 129.9 %score_window.1 = f32[8,384]{1,0:T(8,128)} custom-call(bf16[384,1024]{1,0:T(8,128)(2,1)} %xin.1, bf16[384,1024]{1,0:T(8,128)(2,1)} %gate_in.1, bf16[544,1024]{1,0:T(8,128)(2,1)} %select_in.1, bf16[512,1024]{1,0:T(8,128)(2,1)} %stepw_in.1, bf16[1024,4096]{1,0:T(8,128)(2,1)} %outw_in.1, bf16[256,2048]{1,0:T(8,128)(2,1)} %head_in.1, bf16[384,256]{1,0:T(8,128)(2,1)} %residual.1, ...), custom_call_target="tpu_custom_call" | custom-call | tf_op jit(solution)/shard_map/score_window/pallas_call | solution.py:580
  131.8 1.4 %slice_reduce_fusion = (f32[384]{0:T(512)}, f32[384]{0:T(512)}, f32[384]{0:T(512)}) fusion(f32[8,384]{1,0:T(8,128)} %score_window.1), kind=kLoop, calls=%fused_computation | loop fusion | bytes 9216 | tf_op jit(solution)/shard_map/slice | solution.py:612

commit v4 on v3

--- a/solution.py
+++ b/solution.py
@@ -168,7 +168,8 @@
 
     local[1].wait()
     sends1 = {}
-    for t in range(NT):
+
+    def convolve(t):
         for k in range(TC // 32):
             r0 = TC * t + 32 * k
             for half in range(2):
@@ -177,6 +178,9 @@
                 for offset in range(KCONV):
                     v = v + conv_w[offset : offset + 1, lanes] * xpad[r0 + 5 + offset : r0 + 37 + offset, lanes]
                 sm[r0 : r0 + 32, lanes] = sigmoid_linear(v).astype(BF16)
+
+    for t in range(NT):
+        pl.when(ch >= 0)(lambda: convolve(t))
         product = lax.dot_general(
             sel[...], sm[TC * t : TC * t + TC, :], (((1,), (1,)), ((), ())), preferred_element_type=F32
         )
@@ -442,10 +446,29 @@
 
         def logit(j, held):
             where = pl.ds(pl.multiple_of(j * VT, VT), VT)
-            acc[j, here] = jnp.dot(scaled[here, :], head[:, where], preferred_element_type=F32) * rms[here, :]
+            value = None
+            for i in (0, 1, 7, 2, 6, 3, 5):
+                product = chip_part(here, where, i)
+                value = product if value is None else value + product
+            acc[j, here] = value
             return held
 
         lax.fori_loop(0, NVT, logit, 0)
+
+    def chip_part(here, where, i):
+        deep = pl.ds(pl.multiple_of(lax.rem(z + i, NZ) * 2 * HB, 2 * HB), 2 * HB)
+        return jnp.dot(scaled[here, deep], head[deep, where], preferred_element_type=F32)
+
+    def last_part(j, held):
+        where = pl.ds(pl.multiple_of(j * VT, VT), VT)
+        acc[j] = (acc[j] + chip_part(slice(0, TOK), where, 4)) * rms[...]
+        return held
+
+    def shared(k, p):
+        for way in range(2):
+            if valid(way, k, p):
+                where = head.at[pl.ds(0, HP)]
+                remote(where, where, hps.at[way, k, p], hpr.at[way, k, p], partner).wait_recv()
 
     gate_chunk(0)
     local[5].wait()
@@ -456,36 +479,35 @@
     multiply(1)
     fold(0, 1)
     fold(1, 0)
-    pump(2, 0)
     fold(0, 2)
     fold(1, 1)
     finish(0)
+    pump(2, 0)
     fold(1, 2)
-    pump(2, 1)
     widen(0, 0)
     finish(1)
     widen(0, 1)
+    pump(2, 1)
     widen(1, 0)
     widen(0, 2)
     widen(1, 1)
     widen(1, 2)
     widen(0, 3)
-    for p in range(2):
-        pump(3, p)
 
     local[4].wait()
-    for k in range(4):
+    for k in range(3):
         for p in range(2):
-            for way in range(2):
-                if valid(way, k, p):
-                    where = head.at[pl.ds(0, HP)]
-                    remote(where, where, hps.at[way, k, p], hpr.at[way, k, p], partner).wait_recv()
+            shared(k, p)
     remote(head_in, mine_rows, hps.at[0, 3, 1], hpr.at[0, 3, 1], partner).wait_recv()
-
     logits(0)
     widen(1, 3)
     logits(1)
-    tcol[...] = jnp.transpose(jnp.broadcast_to((targets[...] - ch * VOC).astype(F32), (128, TOK)))
+    for p in range(2):
+        pump(3, p)
+    for p in range(2):
+        shared(3, p)
+    lax.fori_loop(0, NVT, last_part, 0)
+    tcol[...] = jnp.transpose(jnp.broadcast_to((targets[...].reshape(1, TOK) - ch * VOC).astype(F32), (128, TOK)))
     lane = lax.broadcasted_iota(jnp.int32, (32, VT), 1).astype(F32)
     place = lax.broadcasted_iota(jnp.int32, (32, 128), 1)
 
@@ -607,7 +629,7 @@
         name="score_window",
     )(
         layer_input, gate_input, select_weight, step_weight, out_weight, head_weight, residual, conv_weight,
-        conv_bias[None, :], step_bias[None, :], decay_log, skip_gain[None, :], norm_gain[None, :], targets[None, :],
+        conv_bias[None, :], step_bias[None, :], decay_log, skip_gain[None, :], norm_gain[None, :], targets,
     )
     return result[0], result[1], result[2]
 

time: 133 us -> 132 us (level)
  no operation moved by 1% of the time
where the time goes in v4:
time: 132 us
  Pallas kernels  130 us (98%)
  local copies, waits for them, and re-layouts  1.42 us (1%)
    pallas_call x1, Pallas kernels, per_device(): pl.pallas_call(kernel, out_shape=jax.ShapeDtypeStruct((8, TOK), F32), in_...  130 us

profile of v4, /device:TPU:1, one launch (start us, length us, event | category | flops | bytes accessed | tf_op | source)
XLA Modules:
  0.0 131.7 jit_solution(11961011007389084160)
XLA Ops:
  0.6 129.6 %score_window.1 = f32[8,384]{1,0:T(8,128)} custom-call(bf16[384,1024]{1,0:T(8,128)(2,1)} %xin.1, bf16[384,1024]{1,0:T(8,128)(2,1)} %gate_in.1, bf16[544,1024]{1,0:T(8,128)(2,1)} %select_in.1, bf16[512,1024]{1,0:T(8,128)(2,1)} %stepw_in.1, bf16[1024,4096]{1,0:T(8,128)(2,1)} %outw_in.1, bf16[256,2048]{1,0:T(8,128)(2,1)} %head_in.1, bf16[384,256]{1,0:T(8,128)(2,1)} %residual.1, ...), custom_call_target="tpu_custom_call" | custom-call | tf_op jit(solution)/shard_map/score_window/pallas_call | solution.py:602
  130.2 1.4 %slice_reduce_fusion = (f32[384]{0:T(512)}, f32[384]{0:T(512)}, f32[384]{0:T(512)}) fusion(f32[8,384]{1,0:T(8,128)} %score_window.1), kind=kLoop, calls=%fused_computation | loop fusion | bytes 9216 | tf_op jit(solution)/shard_map/slice | solution.py:634
